TPU v7x, 256 devices: a whole 4x4x8 slice. The times are simulated.
256 devices in a mesh: samp: 64 (over z, x, core), snp: 4 (over y).
Axes of the slice: x: 4, y: 4, z: 8, core: 2. Of those that a mesh axis runs over, the one named last changes fastest.
Arguments:
- genotype: int32 [40960, 4096], P('samp', 'snp'), may hold values from 0 to 2
- freqs: float32 [4096], P('snp'), may hold values from 0.35 to 0.65
- left_factors: float32 [40960, 20], P('samp'), may hold values from -6 to 6
- singular: float32 [20], replicated, may hold values from 0.5 to 2
- right_factors: float32 [4096, 20], P(('snp', 'samp')), may hold values from -1.25 to 1.25
- sketch: bfloat16 [4096, 64], P('snp'), may hold values from -6 to 6
- batch_sizes: int32 [12], replicated, may hold values from 1 to 6826, 40960 in all
- missing_batch: int32 [48], replicated, may hold values from 0 to 11, as said below
- missing_block: int32 [48], replicated, may hold values from 0 to 15, as said below
Outputs:
- basis: float32 [40960, 64], P('samp')
- projection: float32 [4096, 64], P('snp')
- snp_basis: float32 [4096, 64], P('snp')
Inputs may be any that keep to these rules, and one draw needn't show every extreme that they name: The pairs (missing_batch, missing_block) are distinct; every block id appears exactly 3 times and every batch id exactly 48 // 12 times. `missing_block`: paired entry by entry with missing_batch.
All inputs are finite; a program needn't handle non-finite values.
Results may differ from a plain program's by a relative error of at most 0.012.
Values may be sent and summed in bfloat16 or wider, within the bound.
No kernel may reach another device: no remote copies, remote signals or barrier semaphores. Data moves between devices by JAX's collectives and lax.ppermute only.
A program may use at most 64 MiB of HBM per device.

v0:
```python
import math

import jax
import jax.numpy as jnp
from jax import lax
from jax.sharding import PartitionSpec as P

BATCHES = 12
BLOCK = 256
ITERS = 2
BLOCKS = 16


def finish_basis(values, gram):
    lower = jnp.linalg.cholesky(gram)
    return jax.scipy.linalg.solve_triangular(lower, values.T, lower=True).T


def reversed_basis(values, gram):
    flipped = finish_basis(values[:, ::-1], gram[::-1, ::-1])
    return flipped[:, ::-1]


def own_gram(values):
    return jnp.dot(values.T, values, precision=lax.Precision.HIGHEST)


def sample_basis(matrix, right_side, sample_count):
    partial_value = jnp.dot(matrix, right_side, preferred_element_type=jnp.float32)
    summed = lax.psum(partial_value.astype(jnp.bfloat16), "snp").astype(jnp.float32)
    gram = lax.psum(own_gram(summed), "samp") / sample_count
    return finish_basis(summed, gram)


def snp_columns(matrix, basis):
    local_part = lax.dot_general(
        matrix,
        basis.astype(jnp.bfloat16),
        (((0,), (0,)), ((), ())),
        preferred_element_type=jnp.float32,
    )
    return lax.psum(local_part, "samp")


def snp_basis(columns, snp_count):
    gram = lax.psum(own_gram(columns), "snp") / snp_count
    return reversed_basis(columns, gram)


def on_device(
    genotype,
    freqs,
    left_factors,
    singular,
    right_factors,
    sketch,
    batch_sizes,
    missing_batch,
    missing_block,
):
    row_count, col_width = genotype.shape
    sample_count = row_count * lax.axis_size("samp")
    snp_count = col_width * lax.axis_size("snp")
    right_local = lax.all_gather(right_factors, "samp", axis=0, tiled=True)
    batch_range = jnp.arange(BATCHES, dtype=jnp.int32)
    block_range = jnp.arange(BLOCKS, dtype=jnp.int32)
    hot_batch = (missing_batch[:, None] == batch_range[None, :]).astype(jnp.float32)
    hot_block = (missing_block[:, None] == block_range[None, :]).astype(jnp.float32)
    table = jnp.dot(hot_batch.T, hot_block, preferred_element_type=jnp.float32)
    ends = jnp.cumsum(batch_sizes)
    row_ids = lax.axis_index("samp") * row_count + jnp.arange(row_count, dtype=jnp.int32)
    batch_of = jnp.sum((row_ids[:, None] >= ends[None, :]).astype(jnp.int32), axis=1)
    row_hot = (batch_of[:, None] == batch_range[None, :]).astype(jnp.float32)
    col_ids = lax.axis_index("snp") * col_width + jnp.arange(col_width, dtype=jnp.int32)
    col_hot = ((col_ids // BLOCK)[None, :] == block_range[:, None]).astype(jnp.float32)
    missing = (
        jnp.dot(
            jnp.dot(row_hot, table, preferred_element_type=jnp.float32),
            col_hot,
            preferred_element_type=jnp.float32,
        )
        > 0.5
    )
    lowrank = jnp.dot(
        left_factors * singular[None, :], right_local.T, precision=lax.Precision.HIGHEST
    )
    observed = genotype.astype(jnp.float32) - 2.0 * freqs[None, :]
    matrix = jnp.where(missing, lowrank, observed).astype(jnp.bfloat16)
    basis = sample_basis(matrix, sketch, sample_count)
    column_basis = jnp.zeros((col_width, sketch.shape[1]), jnp.float32)
    for sweep_index in range(ITERS):
        column_basis = snp_basis(snp_columns(matrix, basis), snp_count)
        basis = sample_basis(matrix, column_basis.astype(jnp.bfloat16), sample_count)
    projection = snp_columns(matrix, basis) / math.sqrt(sample_count)
    return (basis, projection, column_basis)


def solution(mesh):
    in_specs = (
        P("samp", "snp"),
        P("snp"),
        P("samp", None),
        P(),
        P(("snp", "samp"), None),
        P("snp", None),
        P(),
        P(),
        P(),
    )
    out_specs = (P("samp", None), P("snp", None), P("snp", None))
    return jax.shard_map(
        on_device, mesh=mesh, in_specs=in_specs, out_specs=out_specs, check_vma=False
    )
```

profile of v0, /device:TPU:1, one launch (start us, length us, event | category | flops | bytes accessed | tf_op | source)
XLA Modules:
  0.0 1585.5 jit_solution(2528023982231809789)
XLA Ops:
  7.3 0.7 broadcast_multiply_fusion.6
  8.0 54.6 %all_gather.3 = f32[1024,20]{1,0:T(8,128)S(1)} all-gather(f32[16,20]{1,0:T(8,128)} %param.18), channel_id=1, replica_groups=mesh['samp'=64,'snp'=4] {'samp'}, dimensions={0}, use_global_device_ids=true | all-gather | bytes 83200 | tf_op jit(solution)/shard_map/all_gather | solution.py:64
  62.6 0.8 reduce-window.8
  63.4 0.1 convert_reduce_fusion
  63.5 0.9 fusion.43
  64.4 2.2 fusion
  66.6 5.1 select_convert_fusion
  71.7 1.2 convolution_convert_fusion.2
  72.9 40.8 %all-reduce.7.cloned.1.call-done = bf16[640,64]{0,1:T(8,128)(2,1)} async-done(((bf16[640,64]{0,1:T(8,128)(2,1)}), bf16[640,64]{0,1:T(8,128)(2,1)}) %all-reduce.7.cloned.1.call-update) | async-done | bytes 81936 | tf_op jit(solution)/shard_map/psum | solution.py:30
  113.7 1.1 fusion.49
  114.8 246.0 %psum.78 = f32[64,64]{0,1:T(8,128)S(1)} all-reduce(f32[64,64]{0,1:T(8,128)S(1)} %fusion.49), channel_id=1, replica_groups=mesh['samp'=64,'snp'=4] {'samp'}, use_global_device_ids=true, to_apply=%region_3.4 | all-reduce | flops 4096 | bytes 32768 | tf_op jit(solution)/shard_map/psum | solution.py:31
  360.8 0.1 copy.23
  360.9 5.8 cholesky.89
  366.8 0.6 compare_reduce_fusion.4
  367.4 0.7 fusion.18
  368.1 4.9 custom-call.11
  373.0 1.2 convolution_convert_fusion.4
  374.3 1.1 fusion.54
  375.4 176.2 %all-reduce.9.cloned.1.call-done = f32[1024,64]{0,1:T(8,128)} async-done(((f32[1024,64]{0,1:T(8,128)}), f32[1024,64]{0,1:T(8,128)}) %all-reduce.9.cloned.1.call-update) | async-done | bytes 262160 | tf_op jit(solution)/shard_map/psum | solution.py:42
  551.6 1.4 fusion.50
  553.0 0.1 reverse.6
  553.1 13.3 psum.80
  566.5 5.8 cholesky.100
  572.4 0.6 compare_reduce_fusion.3
  573.0 0.7 fusion.19
  573.7 4.9 custom-call.12
  578.6 3.1 rev.19
  581.6 0.4 convolution_bitcast_fusion.1
  582.1 0.3 rev.20
  582.3 1.2 convolution_convert_fusion.1
  583.5 0.2 all-reduce.13.cloned.1.call-start
  583.7 42.7 %all-reduce.11.cloned.1.call-done = bf16[640,64]{0,1:T(8,128)(2,1)} async-done(((bf16[640,64]{0,1:T(8,128)(2,1)}), bf16[640,64]{0,1:T(8,128)(2,1)}) %all-reduce.11.cloned.1.call-update) | async-done | bytes 81936 | tf_op jit(solution)/shard_map/psum | solution.py:30
  626.4 1.1 fusion.51
  627.5 246.0 %psum.82 = f32[64,64]{0,1:T(8,128)S(1)} all-reduce(f32[64,64]{0,1:T(8,128)S(1)} %fusion.51), channel_id=1, replica_groups=mesh['samp'=64,'snp'=4] {'samp'}, use_global_device_ids=true, to_apply=%region_9.13 | all-reduce | flops 4096 | bytes 32768 | tf_op jit(solution)/shard_map/psum | solution.py:31
  873.5 0.1 copy.27
  873.6 5.8 cholesky.111
  879.5 0.6 compare_reduce_fusion.2
  880.1 0.7 fusion.20
  880.8 4.9 custom-call.13
  885.7 1.2 convolution_convert_fusion.3
  886.9 1.1 fusion.55
  888.1 176.2 %all-reduce.13.cloned.1.call-done = f32[1024,64]{0,1:T(8,128)} async-done(((f32[1024,64]{0,1:T(8,128)}), f32[1024,64]{0,1:T(8,128)}) %all-reduce.13.cloned.1.call-update) | async-done | bytes 262160 | tf_op jit(solution)/shard_map/psum | solution.py:42
  1064.3 1.4 fusion.52
  1065.7 0.1 reverse.7
  1065.8 13.3 psum.84
  1079.2 5.8 cholesky.122
  1085.1 0.6 compare_reduce_fusion.1
  1085.7 0.7 fusion.21
  1086.4 4.9 custom-call.14
  1091.3 3.1 rev.22
  1094.4 0.4 convolution_bitcast_fusion
  1094.8 0.2 rev.23
  1095.0 1.2 convolution_convert_fusion
  1096.2 42.8 %all-reduce.15.cloned.1.call-done = bf16[640,64]{0,1:T(8,128)(2,1)} async-done(((bf16[640,64]{0,1:T(8,128)(2,1)}), bf16[640,64]{0,1:T(8,128)(2,1)}) %all-reduce.15.cloned.1.call-update) | async-done | bytes 81936 | tf_op jit(solution)/shard_map/psum | solution.py:30
  1139.1 1.1 fusion.53
  1140.2 246.0 %psum.86 = f32[64,64]{0,1:T(8,128)S(1)} all-reduce(f32[64,64]{0,1:T(8,128)S(1)} %fusion.53), channel_id=1, replica_groups=mesh['samp'=64,'snp'=4] {'samp'}, use_global_device_ids=true, to_apply=%region_13.17 | all-reduce | flops 4096 | bytes 32768 | tf_op jit(solution)/shard_map/psum | solution.py:31
  1386.3 5.8 cholesky.133
  1392.2 0.6 compare_reduce_fusion
  1392.8 0.7 fusion.22
  1393.5 4.9 custom-call.15
  1398.4 1.2 convolution_bitcast_fusion.2
  1399.6 1.1 fusion.15
  1400.7 176.2 %all-reduce.17.cloned.1.call-done = f32[1024,64]{0,1:T(8,128)} async-done(((f32[1024,64]{0,1:T(8,128)}), f32[1024,64]{0,1:T(8,128)}) %all-reduce.17.cloned.1.call-update) | async-done | bytes 262160 | tf_op jit(solution)/shard_map/psum | solution.py:42
  1576.9 1.7 broadcast_multiply_fusion
  (41 shorter events, 0.8 us)
Async XLA Ops:
  7.2 64.5 %copy-start = (bf16[1024,64]{0,1:T(8,128)(2,1)S(1)}, bf16[1024,64]{0,1:T(8,128)(2,1)}, u32[]{:S(2)}) copy-start(bf16[1024,64]{0,1:T(8,128)(2,1)} %param.19) | copy-start | bytes 393220
  7.2 106.5 %all-reduce.7.cloned.1.call-start = ((), (), s32[]{:S(2)}) async-start(), calls=%async_computation | async-start | bytes 163840 | tf_op jit(solution)/shard_map/psum | solution.py:30
  64.4 2.2 copy-start.3
  64.4 2.2 copy-start.4
  72.9 478.7 %all-reduce.9.cloned.1.call-start = ((), (), s32[]{:S(2)}) async-start(), calls=%async_computation.1 | async-start | bytes 524288 | tf_op jit(solution)/shard_map/psum | solution.py:42
  375.3 251.1 %all-reduce.11.cloned.1.call-start = ((), (), s32[]{:S(2)}) async-start(), calls=%async_computation.2 | async-start | bytes 163840 | tf_op jit(solution)/shard_map/psum | solution.py:30
  583.5 480.8 %all-reduce.13.cloned.1.call-start = ((), (), s32[]{:S(2)}) async-start(), calls=%async_computation.3 | async-start | bytes 524288 | tf_op jit(solution)/shard_map/psum | solution.py:42
  888.0 251.0 %all-reduce.15.cloned.1.call-start = ((), (), s32[]{:S(2)}) async-start(), calls=%async_computation.4 | async-start | bytes 163840 | tf_op jit(solution)/shard_map/psum | solution.py:30
  1095.0 305.7 %copy-start.1 = (f32[1024,64]{0,1:T(8,128)}, f32[1024,64]{0,1:T(8,128)S(1)}, u32[]{:S(2)}) copy-start(f32[1024,64]{0,1:T(8,128)S(1)} %rev.23) | copy-start | bytes 786436
  1096.2 480.8 %all-reduce.17.cloned.1.call-start = ((), (), s32[]{:S(2)}) async-start(), calls=%async_computation.5 | async-start | bytes 524288 | tf_op jit(solution)/shard_map/psum | solution.py:42
  1399.6 179.0 %copy-start.2 = (f32[640,64]{0,1:T(8,128)}, f32[640,64]{0,1:T(8,128)S(1)}, u32[]{:S(2)}) copy-start(f32[640,64]{0,1:T(8,128)S(1)} %convolution_bitcast_fusion.2) | copy-start | bytes 491524
Sparse Core Ops, SparseCore 0:
  73.0 40.6 all-reduce.6
  375.5 176.0 all-reduce.8
  583.6 42.7 all-reduce.10
  888.2 176.1 all-reduce.12
  1096.3 42.7 all-reduce.14
  1400.8 176.0 all-reduce.16
where the time goes:
time: 1590 us
  blocking collectives  819 us (52%)
  waiting for transfers between devices  655 us (41%)
  other arithmetic  63.7 us (4%)
  matrix products  25.5 us (2%)
    psum x3, blocking collectives, sample_basis(): gram = lax.psum(own_gram(summed), 'samp') / sample_count  738 us
    psum x3, waiting for transfers between devices, snp_columns(): return lax.psum(local_part, 'samp')  529 us
    psum x3, waiting for transfers between devices, sample_basis(): lax.psum(partial_value.astype(jnp.bfloat16), 'snp').astype(jnp.float32)  126 us
    all_gather x1, blocking collectives, on_device(): right_local = lax.all_gather(right_factors, 'samp', axis=0, tiled=True)  54.6 us
    another operation x15, other arithmetic, finish_basis(): lower = jnp.linalg.cholesky(gram)  32.6 us
  transfers between devices with their start and end apart: 6, of which 6 were waited for; matrix products, arithmetic and copies ran while one was open for 0% of the time, Pallas kernels for 0%

commit v1 on v0

v1 whole, which is shorter than its diff:
```python
import math

import jax
import jax.numpy as jnp
from jax import lax
from jax.sharding import PartitionSpec as P

BATCHES = 12
BLOCK = 256
ITERS = 2
BLOCKS = 16
TILE = (8, 128)
HIGH = lax.Precision.HIGHEST


def exact_dot(a, b, contract):
    return lax.dot_general(a, b, (contract, ((), ())), precision=HIGH)


def split_dot(values, matrix, dim):
    high = values.astype(jnp.bfloat16)
    low = (values - high.astype(jnp.float32)).astype(jnp.bfloat16)
    both = jnp.concatenate([high, low], axis=0)
    out = lax.dot_general(
        both, matrix, (((1,), (dim,)), ((), ())), preferred_element_type=jnp.float32
    )
    rows = values.shape[0]
    return out[:rows] + out[rows:]


def lower_inverse(gram):
    lower = jnp.linalg.cholesky(gram)
    eye = jnp.eye(gram.shape[0], dtype=gram.dtype)
    return jax.scipy.linalg.solve_triangular(lower, eye, lower=True)


def upper_inverse(gram):
    return lower_inverse(gram[::-1, ::-1])[::-1, ::-1]


def snp_sum(value):
    size = lax.axis_size("snp")
    others = [
        lax.ppermute(value, "snp", [(i, (i + k) % size) for i in range(size)])
        for k in range(1, size)
    ]
    for other in others:
        value = value + other
    return value


def samp_sum(columns, gram):
    count = lax.axis_size("samp")
    rows, width = columns.shape
    across = width // TILE[1]
    tiles = columns.reshape(rows // 8, 8, across, 128).transpose(0, 2, 1, 3)
    wide = jnp.pad(gram, ((0, 0), (0, 128 - gram.shape[1])))
    gram_tiles = jnp.broadcast_to(wide.reshape(rows // 8, 1, 8, 128), tiles.shape)
    send = jnp.concatenate([tiles, gram_tiles], axis=2).reshape(count, -1, 16, 128)
    parts = send.shape[1]
    send = send.reshape(count, parts * 16, 128)
    got = lax.all_to_all(send, "samp", 0, 0)
    total = jnp.sum(got, axis=0)
    spread = lax.all_to_all(jnp.broadcast_to(total[None], got.shape), "samp", 0, 0)
    spread = spread.reshape(rows // 8, across, 16, 128)
    columns = spread[:, :, :8].transpose(0, 2, 1, 3).reshape(rows, width)
    gram = spread[:, 0, 8:, : gram.shape[1]].reshape(rows, gram.shape[1])
    return columns, gram


def on_device(
    genotype,
    freqs,
    left_factors,
    singular,
    right_factors,
    sketch,
    batch_sizes,
    missing_batch,
    missing_block,
):
    row_count, col_width = genotype.shape
    samp_size = lax.axis_size("samp")
    sample_count = row_count * samp_size
    snp_count = col_width * lax.axis_size("snp")
    right_local = lax.all_to_all(
        jnp.broadcast_to(right_factors[None], (samp_size, *right_factors.shape)), "samp", 0, 0
    ).reshape(col_width, -1)
    batch_range = jnp.arange(BATCHES, dtype=jnp.int32)
    block_range = jnp.arange(BLOCKS, dtype=jnp.int32)
    hot_batch = (missing_batch[:, None] == batch_range[None, :]).astype(jnp.float32)
    hot_block = (missing_block[:, None] == block_range[None, :]).astype(jnp.float32)
    table = jnp.dot(hot_batch.T, hot_block, preferred_element_type=jnp.float32)
    ends = jnp.cumsum(batch_sizes)
    row_ids = lax.axis_index("samp") * row_count + jnp.arange(row_count, dtype=jnp.int32)
    batch_of = jnp.sum((row_ids[:, None] >= ends[None, :]).astype(jnp.int32), axis=1)
    row_hot = (batch_of[:, None] == batch_range[None, :]).astype(jnp.float32)
    col_ids = lax.axis_index("snp") * col_width + jnp.arange(col_width, dtype=jnp.int32)
    col_hot = ((col_ids // BLOCK)[None, :] == block_range[:, None]).astype(jnp.float32)
    missing = (
        jnp.dot(
            jnp.dot(row_hot, table, preferred_element_type=jnp.float32),
            col_hot,
            preferred_element_type=jnp.float32,
        )
        > 0.5
    )
    lowrank = jnp.dot(left_factors * singular[None, :], right_local.T, precision=HIGH)
    observed = genotype.astype(jnp.float32) - 2.0 * freqs[None, :]
    matrix = jnp.where(missing, lowrank, observed).astype(jnp.bfloat16)

    start = lax.dot_general(
        sketch, matrix, (((0,), (1,)), ((), ())), preferred_element_type=jnp.float32
    )
    samples = snp_sum(start)
    columns = None
    for sweep_index in range(ITERS + 1):
        partial_columns = split_dot(samples, matrix, 0)
        partial_gram = exact_dot(samples, samples, ((1,), (1,)))
        raw, gram = samp_sum(partial_columns, partial_gram)
        factor = lower_inverse(gram / sample_count)
        if sweep_index == ITERS:
            break
        raw = exact_dot(factor, raw, ((1,), (0,)))
        product = split_dot(raw, matrix, 1)
        own = exact_dot(raw, raw, ((1,), (1,)))
        summed = snp_sum(jnp.concatenate([product, own], axis=1))
        factor = upper_inverse(summed[:, row_count:] / snp_count)
        samples = exact_dot(factor, summed[:, :row_count], ((1,), (0,)))
        columns = exact_dot(factor, raw, ((1,), (0,)))
    basis = exact_dot(samples, factor, ((0,), (1,)))
    projection = exact_dot(raw, factor / math.sqrt(sample_count), ((0,), (1,)))
    return (basis, projection, columns.T)


def solution(mesh):
    in_specs = (
        P("samp", "snp"),
        P("snp"),
        P("samp", None),
        P(),
        P(("snp", "samp"), None),
        P("snp", None),
        P(),
        P(),
        P(),
    )
    out_specs = (P("samp", None), P("snp", None), P("snp", None))
    return jax.shard_map(
        on_device, mesh=mesh, in_specs=in_specs, out_specs=out_specs, check_vma=False
    )
```

time: 1590 us -> 297 us (0.19)
  blocking collectives: 819 us -> 114 us
  waiting for transfers between devices: 655 us -> 69.9 us
  starting transfers between devices: 0.43 us -> 26.4 us
    psum x5 -> x0, blocking collectives: 765 us -> none  [the longest x3 738 us: sample_basis(): gram = lax.psum(own_gram(summed), 'samp') / sample_count]
    psum x6 -> x0, waiting for transfers between devices: 655 us -> none  [the longest x3 529 us: snp_columns(): return lax.psum(local_part, 'samp')]
    all_to_all x0 -> x5, blocking collectives: none -> 114 us  [the longest x3 67.5 us: samp_sum(): got = lax.all_to_all(send, 'samp', 0, 0)]
    all_gather x1 -> x0, blocking collectives: 54.6 us -> none  [on_device(): right_local = lax.all_gather(right_factors, 'samp', axis=0, tiled=True)]
    ppermute x0 -> x9, waiting for transfers between devices: none -> 45.6 us  [snp_sum(): lax.ppermute(value, 'snp', [(i, (i + k) % size) for i in range(size)])]
    all_to_all x0 -> x2, waiting for transfers between devices: none -> 24.3 us  [the longest x1 16.6 us: samp_sum(): lax.all_to_all(jnp.broadcast_to(total[None], got.shape), 'samp', 0, 0)]
    all_to_all x0 -> x2, starting transfers between devices: none -> 18.7 us  [the longest x1 13 us: on_device(): lax.all_to_all(jnp.broadcast_to(right_factors[None], (samp_size, *right_f...]
  transfers between devices with their start and end apart: 6 -> 11, of which waited for: 6 -> 11; matrix products, arithmetic and copies ran while one was open for 0% -> 1% of each run, Pallas kernels for 0% -> 0%
where the time goes in v1:
time: 297 us; the launch traced here: 296 us
  blocking collectives  114 us (38%)
  waiting for transfers between devices  69.9 us (24%)
  other arithmetic  62.5 us (21%)
  starting transfers between devices  26.4 us (9%)
  matrix products  18 us (6%)
  local copies, waits for them, and re-layouts  4.34 us (1%)
    all_to_all x3, blocking collectives, samp_sum(): got = lax.all_to_all(send, 'samp', 0, 0)  67.5 us
    all_to_all x2, blocking collectives, samp_sum(): lax.all_to_all(jnp.broadcast_to(total[None], got.shape), 'samp', 0, 0)  46.5 us
    ppermute x9, waiting for transfers between devices, snp_sum(): lax.ppermute(value, 'snp', [(i, (i + k) % size) for i in range(size)])  45.6 us
    another operation x15, other arithmetic, lower_inverse(): lower = jnp.linalg.cholesky(gram)  32.6 us
    another operation x10, other arithmetic, lower_inverse(): return jax.scipy.linalg.solve_triangular(lower, eye, lower=True)  27.7 us
    all_to_all x1, waiting for transfers between devices, samp_sum(): lax.all_to_all(jnp.broadcast_to(total[None], got.shape), 'samp', 0, 0)  16.6 us
    all_to_all x1, starting transfers between devices, on_device(): lax.all_to_all(jnp.broadcast_to(right_factors[None], (samp_size, *right_f...  13 us
    all_to_all x1, waiting for transfers between devices, on_device(): lax.all_to_all(jnp.broadcast_to(right_factors[None], (samp_size, *right_f...  7.67 us
  transfers between devices with their start and end apart: 11, of which 11 were waited for; matrix products, arithmetic and copies ran while one was open for 1% of the time, Pallas kernels for 0%

profile of v1, /device:TPU:1, one launch (start us, length us, event | category | flops | bytes accessed | tf_op | source)
XLA Modules:
  0.0 296.3 jit_solution(3650214405666601010)
XLA Ops:
  0.7 0.8 broadcast_in_dim.20
  1.4 1.0 reshape.125
  2.5 13.0 %all-to-all-start = ((f32[64,1,320]{2,1,0:T(1,128)}), f32[64,1,320]{2,1,0:T(1,128)S(1)}, u32[]{:S(2)}, u32[]{:S(2)}) async-start(f32[64,1,320]{2,1,0:T(1,128)} %reshape.125), calls=%async_computation | async-start | bytes 196608 | tf_op jit(solution)/shard_map/all_to_all | solution.py:86
  16.1 2.3 fusion
  18.4 7.7 %all-to-all-done = f32[64,1,320]{2,1,0:T(1,128)S(1)} async-done(((f32[64,1,320]{2,1,0:T(1,128)}), f32[64,1,320]{2,1,0:T(1,128)S(1)}, u32[]{:S(2)}, u32[]{:S(2)}) %all-to-all-start) | async-done | bytes 81952 | tf_op jit(solution)/shard_map/all_to_all | solution.py:86
  26.0 0.5 broadcast.127
  26.5 0.9 reduce.4
  27.8 5.1 %select_convert_fusion = bf16[640,1024]{1,0:T(8,128)(2,1)S(1)} fusion(s32[640,1024]{1,0:T(8,128)} %param.12, f32[640,1024]{1,0:T(8,128)} %fusion, f32[1024,20]{1,0:T(8,128)S(1)} %bitcast.132, f32[1024]{0:T(1024)S(1)} %broadcast_multiply_fusion.2, f32[640,20]{0,1:T(8,128)S(1)} %copy-done.1, f32[20]{0:T(128)S(1)} %copy-done.3), kind=kOutput, calls=%fused_computation | convolution fusion | flops 160576000 | bytes 6690896 | tf_op jit(solution)/shard_map/dot_general | solution.py:108
  32.9 0.5 convolution_bitcast_fusion
  33.4 2.8 collective-permute-start.2
  36.6 0.7 collective-permute-start
  37.3 5.5 %collective-permute-done.2 = f32[64,640]{1,0:T(8,128)S(1)} collective-permute-done((f32[64,640]{1,0:T(8,128)S(1)}, f32[64,640]{1,0:T(8,128)S(1)}, u32[]{:S(2)}, u32[]{:S(2)}) %collective-permute-start.2) | collective-permute-done | bytes 163872 | tf_op jit(solution)/shard_map/ppermute | solution.py:44
  42.8 4.5 %collective-permute-done = f32[64,640]{1,0:T(8,128)S(1)} collective-permute-done((f32[64,640]{1,0:T(8,128)S(1)}, f32[64,640]{1,0:T(8,128)S(1)}, u32[]{:S(2)}, u32[]{:S(2)}) %collective-permute-start) | collective-permute-done | bytes 163872 | tf_op jit(solution)/shard_map/ppermute | solution.py:44
  47.7 0.4 fusion.21
  48.2 21.6 %all_to_all.35 = f32[64,16,128]{2,1,0:T(8,128)S(1)} all-to-all(f32[64,16,128]{2,1,0:T(8,128)S(1)} %bitcast.133), channel_id=1, replica_groups=mesh['samp'=64,'snp'=4] {'samp'}, dimensions={0} | all-to-all | bytes 1048576 | tf_op jit(solution)/shard_map/all_to_all | solution.py:62
  69.9 23.2 %all_to_all.36 = f32[64,16,128]{2,1,0:T(8,128)S(1)} all-to-all(f32[64,16,128]{2,1,0:T(8,128)S(1)} %broadcast_in_dim.23), channel_id=1, replica_groups=mesh['samp'=64,'snp'=4] {'samp'}, dimensions={0} | all-to-all | bytes 1048576 | tf_op jit(solution)/shard_map/all_to_all | solution.py:64
  93.2 5.8 %cholesky.89 = f32[64,64]{1,0:T(8,128)S(1)} custom-call(f32[64,64]{1,0:T(8,128)S(1)} %fusion.63), custom_call_target="Cholesky" | custom-call | tf_op jit(solution)/shard_map/jit(cholesky)/cholesky | solution.py:32
  99.1 0.6 compare_reduce_fusion.4
  99.8 0.7 fusion.46
  100.4 4.9 %custom-call.9 = f32[1,64,64]{1,2,0:T(8,128)S(1)} custom-call(f32[1,64,64]{2,1,0:T(8,128)S(1)} %fusion.46), custom_call_target="InvertDiagBlocksLowerTriangular" | custom-call | tf_op jit(solution)/shard_map/jit(_solve_triangular)/triangular_solve | solution.py:34
  106.3 0.5 fusion.13
  107.0 0.4 collective-permute-start.4
  107.5 0.9 collective-permute-start.5
  108.4 0.6 collective-permute-start.3
  108.9 9.3 %collective-permute-done.4 = f32[64,704]{0,1:T(8,128)S(1)} collective-permute-done((f32[64,704]{0,1:T(8,128)S(1)}, f32[64,704]{0,1:T(8,128)S(1)}, u32[]{:S(2)}, u32[]{:S(2)}) %collective-permute-start.4) | collective-permute-done | bytes 180256 | tf_op jit(solution)/shard_map/ppermute | solution.py:44
  118.2 5.7 %collective-permute-done.5 = f32[64,704]{0,1:T(8,128)S(1)} collective-permute-done((f32[64,704]{0,1:T(8,128)S(1)}, f32[64,704]{0,1:T(8,128)S(1)}, u32[]{:S(2)}, u32[]{:S(2)}) %collective-permute-start.5) | collective-permute-done | bytes 180256 | tf_op jit(solution)/shard_map/ppermute | solution.py:44
  123.9 2.7 collective-permute-done.3
  126.9 5.8 %cholesky.100 = f32[64,64]{1,0:T(8,128)S(1)} custom-call(f32[64,64]{1,0:T(8,128)S(1)} %fusion.61), custom_call_target="Cholesky" | custom-call | tf_op jit(solution)/shard_map/jit(cholesky)/cholesky | solution.py:32
  132.8 0.6 compare_reduce_fusion.3
  133.5 0.7 fusion.47
  134.1 4.9 %custom-call.10 = f32[1,64,64]{1,2,0:T(8,128)S(1)} custom-call(f32[1,64,64]{2,1,0:T(8,128)S(1)} %fusion.47), custom_call_target="InvertDiagBlocksLowerTriangular" | custom-call | tf_op jit(solution)/shard_map/jit(_solve_triangular)/triangular_solve | solution.py:34
  139.4 0.5 subtract_convert_fusion.3
  140.2 0.4 fusion.25
  140.7 23.0 %all_to_all.37 = f32[64,16,128]{2,1,0:T(8,128)S(1)} all-to-all(f32[64,16,128]{2,1,0:T(8,128)S(1)} %bitcast.134), channel_id=1, replica_groups=mesh['samp'=64,'snp'=4] {'samp'}, dimensions={0} | all-to-all | bytes 1048576 | tf_op jit(solution)/shard_map/all_to_all | solution.py:62
  163.8 23.2 %all_to_all.38 = f32[64,16,128]{2,1,0:T(8,128)S(1)} all-to-all(f32[64,16,128]{2,1,0:T(8,128)S(1)} %broadcast_in_dim.27), channel_id=1, replica_groups=mesh['samp'=64,'snp'=4] {'samp'}, dimensions={0} | all-to-all | bytes 1048576 | tf_op jit(solution)/shard_map/all_to_all | solution.py:64
  187.1 5.8 %cholesky.111 = f32[64,64]{1,0:T(8,128)S(1)} custom-call(f32[64,64]{1,0:T(8,128)S(1)} %fusion.59), custom_call_target="Cholesky" | custom-call | tf_op jit(solution)/shard_map/jit(cholesky)/cholesky | solution.py:32
  193.0 0.6 compare_reduce_fusion.2
  193.6 0.7 fusion.48
  194.3 4.9 %custom-call.11 = f32[1,64,64]{1,2,0:T(8,128)S(1)} custom-call(f32[1,64,64]{2,1,0:T(8,128)S(1)} %fusion.48), custom_call_target="InvertDiagBlocksLowerTriangular" | custom-call | tf_op jit(solution)/shard_map/jit(_solve_triangular)/triangular_solve | solution.py:34
  199.4 0.4 subtract_convert_fusion
  200.2 0.5 fusion.17
  200.9 0.4 collective-permute-start.7
  201.3 0.9 collective-permute-start.8
  202.3 0.5 collective-permute-start.6
  202.8 9.3 %collective-permute-done.7 = f32[64,704]{0,1:T(8,128)S(1)} collective-permute-done((f32[64,704]{0,1:T(8,128)S(1)}, f32[64,704]{0,1:T(8,128)S(1)}, u32[]{:S(2)}, u32[]{:S(2)}) %collective-permute-start.7) | collective-permute-done | bytes 180256 | tf_op jit(solution)/shard_map/ppermute | solution.py:44
  212.1 5.7 %collective-permute-done.8 = f32[64,704]{0,1:T(8,128)S(1)} collective-permute-done((f32[64,704]{0,1:T(8,128)S(1)}, f32[64,704]{0,1:T(8,128)S(1)}, u32[]{:S(2)}, u32[]{:S(2)}) %collective-permute-start.8) | collective-permute-done | bytes 180256 | tf_op jit(solution)/shard_map/ppermute | solution.py:44
  217.8 2.7 collective-permute-done.6
  220.8 5.8 %cholesky.122 = f32[64,64]{1,0:T(8,128)S(1)} custom-call(f32[64,64]{1,0:T(8,128)S(1)} %fusion.57), custom_call_target="Cholesky" | custom-call | tf_op jit(solution)/shard_map/jit(cholesky)/cholesky | solution.py:32
  226.7 0.6 compare_reduce_fusion.1
  227.3 0.7 fusion.49
  228.0 4.9 %custom-call.12 = f32[1,64,64]{1,2,0:T(8,128)S(1)} custom-call(f32[1,64,64]{2,1,0:T(8,128)S(1)} %fusion.49), custom_call_target="InvertDiagBlocksLowerTriangular" | custom-call | tf_op jit(solution)/shard_map/jit(_solve_triangular)/triangular_solve | solution.py:34
  233.2 0.5 subtract_convert_fusion.2
  233.7 0.4 fusion.29
  234.5 23.0 %all_to_all.39 = f32[64,16,128]{2,1,0:T(8,128)S(1)} all-to-all(f32[64,16,128]{2,1,0:T(8,128)S(1)} %bitcast.135), channel_id=1, replica_groups=mesh['samp'=64,'snp'=4] {'samp'}, dimensions={0} | all-to-all | bytes 1048576 | tf_op jit(solution)/shard_map/all_to_all | solution.py:62
  257.6 0.8 broadcast_in_dim.30
  258.4 5.7 %all-to-all-start.6 = ((f32[64,16,128]{2,1,0:T(8,128)}), f32[64,16,128]{2,1,0:T(8,128)S(1)}, u32[]{:S(2)}, u32[]{:S(2)}) async-start(f32[64,16,128]{2,1,0:T(8,128)} %broadcast_in_dim.30), calls=%async_computation.6 | async-start | bytes 1048576 | tf_op jit(solution)/shard_map/all_to_all | solution.py:64
  264.1 1.1 fusion.92
  265.2 16.6 %all-to-all-done.6 = f32[64,16,128]{2,1,0:T(8,128)S(1)} async-done(((f32[64,16,128]{2,1,0:T(8,128)}), f32[64,16,128]{2,1,0:T(8,128)S(1)}, u32[]{:S(2)}, u32[]{:S(2)}) %all-to-all-start.6) | async-done | bytes 524320 | tf_op jit(solution)/shard_map/all_to_all | solution.py:64
  282.0 5.8 %cholesky.133 = f32[64,64]{1,0:T(8,128)S(1)} custom-call(f32[64,64]{1,0:T(8,128)S(1)} %fusion.55), custom_call_target="Cholesky" | custom-call | tf_op jit(solution)/shard_map/jit(cholesky)/cholesky | solution.py:32
  287.8 0.6 compare_reduce_fusion
  288.5 0.7 fusion.50
  289.1 4.9 %custom-call.13 = f32[1,64,64]{1,2,0:T(8,128)S(1)} custom-call(f32[1,64,64]{2,1,0:T(8,128)S(1)} %fusion.50), custom_call_target="InvertDiagBlocksLowerTriangular" | custom-call | tf_op jit(solution)/shard_map/jit(_solve_triangular)/triangular_solve | solution.py:34
  294.3 1.1 fusion.7
  295.4 1.0 fusion.91
  (84 shorter events, 6.6 us)
Async XLA Ops:
  0.6 32.2 %copy-start = (bf16[1024,64]{0,1:T(8,128)(2,1)S(1)}, bf16[1024,64]{0,1:T(8,128)(2,1)}, u32[]{:S(2)}) copy-start(bf16[1024,64]{0,1:T(8,128)(2,1)} %param.17) | copy-start | bytes 393220
  0.6 14.9 %copy-start.4 = (s32[12]{0:T(128)S(1)}, s32[12]{0:T(128)}, u32[]{:S(2)}) copy-start(s32[12]{0:T(128)} %param.18) | copy-start | bytes 148
  0.7 15.1 %copy-start.5 = (s32[48]{0:T(128)S(1)}, s32[48]{0:T(128)}, u32[]{:S(2)}) copy-start(s32[48]{0:T(128)} %param.20) | copy-start | bytes 580
  0.7 15.1 %copy-start.6 = (s32[48]{0:T(128)S(1)}, s32[48]{0:T(128)}, u32[]{:S(2)}) copy-start(s32[48]{0:T(128)} %param.19) | copy-start | bytes 580
  2.5 23.6 %all-to-all-start = ((f32[64,1,320]{2,1,0:T(1,128)}), f32[64,1,320]{2,1,0:T(1,128)S(1)}, u32[]{:S(2)}, u32[]{:S(2)}) async-start(f32[64,1,320]{2,1,0:T(1,128)} %reshape.125), calls=%async_computation | async-start | bytes 196608 | tf_op jit(solution)/shard_map/all_to_all | solution.py:86
  16.1 2.3 copy-start.2
  16.1 11.7 %copy-start.1 = (f32[640,20]{0,1:T(8,128)S(1)}, f32[640,20]{0,1:T(8,128)}, u32[]{:S(2)}) copy-start(f32[640,20]{0,1:T(8,128)} %param.14) | copy-start | bytes 153604
  16.1 11.7 %copy-start.3 = (f32[20]{0:T(128)S(1)}, f32[20]{0:T(128)}, u32[]{:S(2)}) copy-start(f32[20]{0:T(128)} %param.15) | copy-start | bytes 244
  33.4 9.4 %collective-permute-start.2 = (f32[64,640]{1,0:T(8,128)S(1)}, f32[64,640]{1,0:T(8,128)S(1)}, u32[]{:S(2)}, u32[]{:S(2)}) collective-permute-start(f32[64,640]{1,0:T(8,128)S(1)} %convolution_bitcast_fusion), channel_id=1, source_target_pairs={{0,3},{1,0},{2,1},{3,2},{4,7},{5,4},{6,5},{7,6},{8,11},{9,8},{10,9... | collective-permute-start | bytes 491528 | tf_op jit(solution)/shard_map/ppermute | solution.py:44
  36.2 6.6 %collective-permute-start.1 = (f32[64,640]{1,0:T(8,128)S(1)}, f32[64,640]{1,0:T(8,128)S(1)}, u32[]{:S(2)}, u32[]{:S(2)}) collective-permute-start(f32[64,640]{1,0:T(8,128)S(1)} %convolution_bitcast_fusion), channel_id=1, source_target_pairs={{0,2},{1,3},{2,0},{3,1},{4,6},{5,7},{6,4},{7,5},{8,10},{9,11},{10,... | collective-permute-start | bytes 491528 | tf_op jit(solution)/shard_map/ppermute | solution.py:44
  36.6 10.8 %collective-permute-start = (f32[64,640]{1,0:T(8,128)S(1)}, f32[64,640]{1,0:T(8,128)S(1)}, u32[]{:S(2)}, u32[]{:S(2)}) collective-permute-start(f32[64,640]{1,0:T(8,128)S(1)} %convolution_bitcast_fusion), channel_id=1, source_target_pairs={{0,1},{1,2},{2,3},{3,0},{4,5},{5,6},{6,7},{7,4},{8,9},{9,10},{10,1... | collective-permute-start | bytes 491528 | tf_op jit(solution)/shard_map/ppermute | solution.py:44
  107.0 11.2 %collective-permute-start.4 = (f32[64,704]{0,1:T(8,128)S(1)}, f32[64,704]{0,1:T(8,128)S(1)}, u32[]{:S(2)}, u32[]{:S(2)}) collective-permute-start(f32[64,704]{0,1:T(8,128)S(1)} %pad_maximum_fusion.3), channel_id=1, source_target_pairs={{0,2},{1,3},{2,0},{3,1},{4,6},{5,7},{6,4},{7,5},{8,10},{9,11},{10,... | collective-permute-start | bytes 540680 | tf_op jit(solution)/shard_map/ppermute | solution.py:44
  107.5 16.5 %collective-permute-start.5 = (f32[64,704]{0,1:T(8,128)S(1)}, f32[64,704]{0,1:T(8,128)S(1)}, u32[]{:S(2)}, u32[]{:S(2)}) collective-permute-start(f32[64,704]{0,1:T(8,128)S(1)} %pad_maximum_fusion.3), channel_id=1, source_target_pairs={{0,3},{1,0},{2,1},{3,2},{4,7},{5,4},{6,5},{7,6},{8,11},{9,8},{10,9... | collective-permute-start | bytes 540680 | tf_op jit(solution)/shard_map/ppermute | solution.py:44
  108.4 18.3 %collective-permute-start.3 = (f32[64,704]{0,1:T(8,128)S(1)}, f32[64,704]{0,1:T(8,128)S(1)}, u32[]{:S(2)}, u32[]{:S(2)}) collective-permute-start(f32[64,704]{0,1:T(8,128)S(1)} %pad_maximum_fusion.3), channel_id=1, source_target_pairs={{0,1},{1,2},{2,3},{3,0},{4,5},{5,6},{6,7},{7,4},{8,9},{9,10},{10,1... | collective-permute-start | bytes 540680 | tf_op jit(solution)/shard_map/ppermute | solution.py:44
  200.9 11.2 %collective-permute-start.7 = (f32[64,704]{0,1:T(8,128)S(1)}, f32[64,704]{0,1:T(8,128)S(1)}, u32[]{:S(2)}, u32[]{:S(2)}) collective-permute-start(f32[64,704]{0,1:T(8,128)S(1)} %pad_maximum_fusion.4), channel_id=1, source_target_pairs={{0,2},{1,3},{2,0},{3,1},{4,6},{5,7},{6,4},{7,5},{8,10},{9,11},{10,... | collective-permute-start | bytes 540680 | tf_op jit(solution)/shard_map/ppermute | solution.py:44
  201.3 16.5 %collective-permute-start.8 = (f32[64,704]{0,1:T(8,128)S(1)}, f32[64,704]{0,1:T(8,128)S(1)}, u32[]{:S(2)}, u32[]{:S(2)}) collective-permute-start(f32[64,704]{0,1:T(8,128)S(1)} %pad_maximum_fusion.4), channel_id=1, source_target_pairs={{0,3},{1,0},{2,1},{3,2},{4,7},{5,4},{6,5},{7,6},{8,11},{9,8},{10,9... | collective-permute-start | bytes 540680 | tf_op jit(solution)/shard_map/ppermute | solution.py:44
  202.3 18.3 %collective-permute-start.6 = (f32[64,704]{0,1:T(8,128)S(1)}, f32[64,704]{0,1:T(8,128)S(1)}, u32[]{:S(2)}, u32[]{:S(2)}) collective-permute-start(f32[64,704]{0,1:T(8,128)S(1)} %pad_maximum_fusion.4), channel_id=1, source_target_pairs={{0,1},{1,2},{2,3},{3,0},{4,5},{5,6},{6,7},{7,4},{8,9},{9,10},{10,1... | collective-permute-start | bytes 540680 | tf_op jit(solution)/shard_map/ppermute | solution.py:44
  258.4 23.4 %all-to-all-start.6 = ((f32[64,16,128]{2,1,0:T(8,128)}), f32[64,16,128]{2,1,0:T(8,128)S(1)}, u32[]{:S(2)}, u32[]{:S(2)}) async-start(f32[64,16,128]{2,1,0:T(8,128)} %broadcast_in_dim.30), calls=%async_computation.6 | async-start | bytes 1048576 | tf_op jit(solution)/shard_map/all_to_all | solution.py:64

commit v2 on v0

v2 whole, which is shorter than its diff:
```python
import math

import jax
import jax.numpy as jnp
from jax import lax
from jax.experimental import pallas as pl
from jax.experimental.pallas import tpu as pltpu
from jax.sharding import Mesh, PartitionSpec as P

BATCHES = 12
BLOCK = 256
ITERS = 2
BLOCKS = 16
LANES = 128
SUB = 8
F32 = jnp.float32
BF16 = jnp.bfloat16
HIGH = lax.Precision.HIGHEST


def exact_dot(a, b, a_dim, b_dim):
    return lax.dot_general(
        a, b, (((a_dim,), (b_dim,)), ((), ())), precision=HIGH, preferred_element_type=F32
    )


def split_dot(values, matrix, dim):
    high = values.astype(BF16)
    low = (values - high.astype(F32)).astype(BF16)
    both = jnp.concatenate([high, low], axis=0)
    out = lax.dot_general(
        both, matrix, (((1,), (dim,)), ((), ())), preferred_element_type=F32
    )
    rows = values.shape[0]
    return out[:rows] + out[rows:]


def inverse_factor(gram, lower):
    size = gram.shape[0]
    across = lax.broadcasted_iota(jnp.int32, (size, size), 1)
    down = lax.broadcasted_iota(jnp.int32, (size, size), 0)
    wide = jnp.concatenate([gram, (across == down).astype(F32)], axis=1)
    count = size // SUB
    shape = (SUB, 2 * size)
    tiles = [wide[SUB * t : SUB * (t + 1)] for t in range(count)]
    sub = lax.broadcasted_iota(jnp.int32, shape, 0)
    step = 1 if lower else -1
    for a in range(count)[::step]:
        active = range(a, count) if lower else range(a + 1)
        cols = {
            t: [
                jnp.broadcast_to(tiles[t][:, SUB * a + k : SUB * a + k + 1], shape)
                for k in range(SUB)
            ]
            for t in active
        }
        scale = jnp.zeros(shape, F32)
        for k in range(SUB)[::step]:
            pivot = jnp.broadcast_to(cols[a][k][k : k + 1], shape)
            inverse = 1.0 / pivot
            scale = jnp.where(sub == k, pivot, scale)
            keep = (sub > k) if lower else (sub < k)
            rest = range(k + 1, SUB) if lower else range(k)
            row = jnp.broadcast_to(tiles[a][k : k + 1], shape) * inverse
            heads = {j: jnp.broadcast_to(cols[a][j][k : k + 1], shape) * inverse for j in rest}
            for t in active:
                column = cols[t][k]
                if t == a:
                    column = jnp.where(keep, column, 0.0)
                tiles[t] = tiles[t] - column * row
                for j in rest:
                    cols[t][j] = cols[t][j] - column * heads[j]
        tiles[a] = tiles[a] * lax.rsqrt(scale)
    return jnp.concatenate(tiles, axis=0)[:, size:]


def kernel_call(body, out_shapes, *operands):
    return pl.pallas_call(
        body,
        out_shape=out_shapes,
        compiler_params=pltpu.CompilerParams(vmem_limit_bytes=48 * 1024 * 1024),
    )(*operands)


def shape_of(shape, dtype=F32):
    return jax.ShapeDtypeStruct(shape, dtype)


def write_send(columns, gram, core, mine, other):
    rows, width = columns.shape
    half = rows // 2
    first = core == 0
    wide = jnp.concatenate([gram, jnp.zeros((rows, LANES - gram.shape[1]), F32)], axis=1)
    for value, low in ((columns, 0), (wide, SUB)):
        top, bottom = value[:half], value[half:]
        kept = jnp.where(first, top, bottom)
        sent = jnp.where(first, bottom, top)
        for ref, part in ((mine, kept), (other, sent)):
            for a in range(half // SUB):
                for b in range(width // LANES):
                    at = LANES * b if low == 0 else 0
                    ref[a * (width // LANES) + b, low : low + SUB, :] = part[
                        SUB * a : SUB * (a + 1), at : at + LANES
                    ]


def read_sum(mine, other, core, width):
    across = width // LANES
    half = mine.shape[0] // across
    halves = []
    for ref in (mine, other):
        value = jnp.concatenate(
            [
                jnp.concatenate([ref[a * across + b, :SUB, :] for b in range(across)], axis=1)
                for a in range(half)
            ],
            axis=0,
        )
        gram = jnp.concatenate([ref[a * across, SUB:, :] for a in range(half)], axis=0)
        halves.append((value, gram))
    first = core == 0
    columns, gram = (
        jnp.concatenate([jnp.where(first, m, o), jnp.where(first, o, m)], axis=0)
        for m, o in zip(*halves)
    )
    return columns, gram[:, : gram.shape[0]]


def spread_kernel(parts, out):
    out[...] = jnp.broadcast_to(jnp.sum(parts[...], axis=0, keepdims=True), out.shape)


def three_parts(value):
    high = value.astype(BF16)
    rest = value - high.astype(F32)
    middle = rest.astype(BF16)
    return [high, middle, (rest - middle.astype(F32)).astype(BF16)]


def solution(mesh):
    samp, snp = mesh.shape["samp"], mesh.shape["snp"]
    chips = samp // 2
    fine = Mesh(mesh.devices.reshape(chips, 2, snp), ("chip", "core", "snp"))

    def swap(value):
        return lax.ppermute(value, "core", [(0, 1), (1, 0)])

    def snp_others(value):
        return [
            lax.ppermute(value, "snp", [(i, (i + k) % snp) for i in range(snp)])
            for k in range(1, snp)
        ]

    def samp_sum(mine, other):
        send = mine + swap(other)
        got = lax.all_to_all(send, "chip", 0, 0)
        spread = kernel_call(spread_kernel, shape_of(got.shape), got)
        whole = lax.all_to_all(spread, "chip", 0, 0)
        return whole, swap(whole)

    def on_device(
        genotype,
        freqs,
        left_factors,
        singular,
        right_factors,
        sketch,
        batch_sizes,
        missing_batch,
        missing_block,
    ):
        row_count, col_width = genotype.shape
        rank = left_factors.shape[1]
        width = sketch.shape[1]
        sample_count = row_count * samp
        snp_count = col_width * snp
        core = lax.axis_index("core")
        place = core.reshape(1).astype(jnp.int32)
        samp_index = lax.axis_index("chip") * 2 + core

        right_mine = lax.all_to_all(
            jnp.broadcast_to(right_factors[None], (chips, *right_factors.shape)), "chip", 0, 0
        )
        right_other = swap(right_mine)

        batch_range = jnp.arange(BATCHES, dtype=jnp.int32)
        local_blocks = col_width // BLOCK
        block_range = lax.axis_index("snp") * local_blocks + jnp.arange(
            local_blocks, dtype=jnp.int32
        )
        ends = jnp.sum(
            jnp.where(batch_range[:, None] <= batch_range[None, :], batch_sizes[:, None], 0), axis=0
        )
        row_ids = samp_index * row_count + jnp.arange(row_count, dtype=jnp.int32)
        batch_of = jnp.sum((row_ids[:, None] >= ends[None, :]).astype(jnp.int32), axis=1)
        missing = jnp.sum(
            (
                (batch_of[:, None, None] == missing_batch[None, None, :])
                & (block_range[None, :, None] == missing_block[None, None, :])
            ).astype(F32),
            axis=2,
        )
        observed = (genotype.astype(F32) - 2.0 * freqs[None, :]).astype(BF16)
        weighted = left_factors * singular[None, :]

        def build_kernel(place, obs, miss, weight, mine, other, omega, x_out, start):
            first = place[0] == 0
            r_mine, r_other = mine[...], other[...]
            low = jnp.where(first, r_mine, r_other)
            high = jnp.where(first, r_other, r_mine)
            right = jnp.stack([low, high], axis=1).reshape(col_width, rank)
            lowrank = exact_dot(weight[...], right, 1, 1)
            pieces = []
            for j in range(local_blocks):
                at = slice(BLOCK * j, BLOCK * (j + 1))
                gone = jnp.broadcast_to(miss[:, j : j + 1], (row_count, BLOCK)) > 0.5
                pieces.append(jnp.where(gone, lowrank[:, at], obs[:, at].astype(F32)))
            x = jnp.concatenate(pieces, axis=1).astype(BF16)
            x_out[...] = x
            start[...] = lax.dot_general(
                omega[...], x, (((1,), (1,)), ((), ())), preferred_element_type=F32
            )

        def call_with_place(body, outs, *operands):
            specs = [pl.BlockSpec(memory_space=pltpu.SMEM)] + [
                pl.BlockSpec(memory_space=pltpu.VMEM) for _ in operands
            ]
            return pl.pallas_call(
                body,
                out_shape=outs,
                in_specs=specs,
                compiler_params=pltpu.CompilerParams(vmem_limit_bytes=48 * 1024 * 1024),
            )(place, *operands)

        matrix, start = call_with_place(
            build_kernel,
            (shape_of((row_count, col_width), BF16), shape_of((width, row_count))),
            observed,
            missing,
            weighted,
            right_mine,
            right_other,
            sketch.T,
        )

        part_shape = shape_of((chips, 2 * SUB, LANES))
        packed = row_count + 3 * width

        def first_kernel(place, own, a, b, c, x, samples_out, mine, other):
            samples = own[...] + a[...] + b[...] + c[...]
            samples_out[...] = samples
            write_send(
                split_dot(samples, x[...], 0),
                exact_dot(samples, samples, 1, 1),
                place[0],
                mine,
                other,
            )

        def forward_kernel(place, mine, other, x, raw_out, product_out, gram_out, wire):
            columns, gram = read_sum(mine, other, place[0], col_width)
            raw = exact_dot(inverse_factor(gram / sample_count, True), columns, 1, 0)
            raw_out[...] = raw
            product = split_dot(raw, x[...], 1)
            own = exact_dot(raw, raw, 1, 1)
            product_out[...] = product
            gram_out[...] = own
            wire[...] = jnp.concatenate([product.astype(BF16), *three_parts(own)], axis=1)

        def backward_kernel(
            place, product, gram, a, b, c, raw, x, samples_out, columns_out, mine, other
        ):
            total, own = product[...], gram[...]
            for ref in (a, b, c):
                total = total + ref[:, :row_count].astype(F32)
                parts = [
                    ref[:, row_count + width * i : row_count + width * (i + 1)].astype(F32)
                    for i in range(3)
                ]
                own = own + (parts[0] + (parts[1] + parts[2]))
            factor = inverse_factor(own / snp_count, False)
            samples = exact_dot(factor, total, 1, 0)
            samples_out[...] = samples
            columns_out[...] = exact_dot(factor, raw[...], 1, 0)
            write_send(
                split_dot(samples, x[...], 0),
                exact_dot(samples, samples, 1, 1),
                place[0],
                mine,
                other,
            )

        def last_kernel(place, mine, other, samples, basis, projection):
            columns, gram = read_sum(mine, other, place[0], col_width)
            factor = inverse_factor(gram / sample_count, True)
            basis[...] = exact_dot(factor, samples[...], 1, 0)
            projection[...] = exact_dot(factor / math.sqrt(sample_count), columns, 1, 0)

        samples_shape = shape_of((width, row_count))
        columns_shape = shape_of((width, col_width))
        samples, mine, other = call_with_place(
            first_kernel,
            (samples_shape, part_shape, part_shape),
            start,
            *snp_others(start),
            matrix,
        )
        columns = None
        for _ in range(ITERS):
            raw, product, gram, wire = call_with_place(
                forward_kernel,
                (
                    columns_shape,
                    samples_shape,
                    shape_of((width, width)),
                    shape_of((width, packed), BF16),
                ),
                *samp_sum(mine, other),
                matrix,
            )
            samples, columns, mine, other = call_with_place(
                backward_kernel,
                (samples_shape, columns_shape, part_shape, part_shape),
                product,
                gram,
                *snp_others(wire),
                raw,
                matrix,
            )
        basis, projection = call_with_place(
            last_kernel, (samples_shape, columns_shape), *samp_sum(mine, other), samples
        )
        return (basis.T, projection.T, columns.T)

    samp_axes = ("chip", "core")
    in_specs = (
        P(samp_axes, "snp"),
        P("snp"),
        P(samp_axes, None),
        P(),
        P(("snp", *samp_axes), None),
        P("snp", None),
        P(),
        P(),
        P(),
    )
    out_specs = (P(samp_axes, None), P("snp", None), P("snp", None))
    return jax.shard_map(
        on_device, mesh=fine, in_specs=in_specs, out_specs=out_specs, check_vma=False
    )
```

time: 1590 us -> 192 us (0.12)
  blocking collectives: 819 us -> 92.1 us
  waiting for transfers between devices: 655 us -> 36.5 us
  other arithmetic: 63.7 us -> 6.15 us
  starting transfers between devices: 0.43 us -> 32.4 us
  matrix products: 25.5 us -> 0 us
  Pallas kernels: 0 us -> 19.7 us
    psum x5 -> x0, blocking collectives: 765 us -> none  [the longest x3 738 us: sample_basis(): gram = lax.psum(own_gram(summed), 'samp') / sample_count]
    psum x6 -> x0, waiting for transfers between devices: 655 us -> none  [the longest x3 529 us: snp_columns(): return lax.psum(local_part, 'samp')]
    all_to_all x0 -> x6, blocking collectives: none -> 92.1 us  [the longest x3 47.1 us: samp_sum(): got = lax.all_to_all(send, 'chip', 0, 0)]
    another operation x26 -> x0, other arithmetic: 61.2 us -> none  [the longest x15 32.6 us: finish_basis(): lower = jnp.linalg.cholesky(gram)]
    all_gather x1 -> x0, blocking collectives: 54.6 us -> none  [on_device(): right_local = lax.all_gather(right_factors, 'samp', axis=0, tiled=True)]
    ppermute x0 -> x16, waiting for transfers between devices: none -> 33.9 us  [the longest x9 26.1 us: snp_others(): lax.ppermute(value, 'snp', [(i, (i + k) % snp) for i in range(snp)])]
    dot_general x14 -> x0, matrix products: 20.9 us -> none  [the longest x5 6.07 us: own_gram(): return jnp.dot(values.T, values, precision=lax.Precision.HIGHEST)]
    ppermute x0 -> x16, starting transfers between devices: none -> 20.4 us  [the longest x7 13.5 us: swap(): return lax.ppermute(value, 'core', [(0, 1), (1, 0)])]
  transfers between devices with their start and end apart: 6 -> 17, of which waited for: 6 -> 17; matrix products, arithmetic and copies ran while one was open for 0% -> 3% of each run, Pallas kernels for 0% -> 0%
where the time goes in v2:
time: 192 us; the launch traced here: 191 us
  blocking collectives  92.1 us (48%)
  waiting for transfers between devices  36.5 us (19%)
  starting transfers between devices  32.4 us (17%)
  Pallas kernels  19.7 us (10%)
  other arithmetic  6.15 us (3%)
  local copies, waits for them, and re-layouts  3.39 us (2%)
    all_to_all x3, blocking collectives, samp_sum(): got = lax.all_to_all(send, 'chip', 0, 0)  47.1 us
    all_to_all x3, blocking collectives, samp_sum(): whole = lax.all_to_all(spread, 'chip', 0, 0)  45 us
    ppermute x9, waiting for transfers between devices, snp_others(): lax.ppermute(value, 'snp', [(i, (i + k) % snp) for i in range(snp)])  26.1 us
    pallas_call x7, Pallas kernels, call_with_place(): pl.pallas_call(body, out_shape=outs, in_specs=specs, compiler_params=pltp...  19.5 us
    ppermute x7, starting transfers between devices, swap(): return lax.ppermute(value, 'core', [(0, 1), (1, 0)])  13.5 us
    all_to_all x1, starting transfers between devices, on_device(): lax.all_to_all(jnp.broadcast_to(right_factors[None], (chips, *right_facto...  12 us
    ppermute x7, waiting for transfers between devices, swap(): return lax.ppermute(value, 'core', [(0, 1), (1, 0)])  7.81 us
    ppermute x9, starting transfers between devices, snp_others(): lax.ppermute(value, 'snp', [(i, (i + k) % snp) for i in range(snp)])  6.89 us
  transfers between devices with their start and end apart: 17, of which 17 were waited for; matrix products, arithmetic and copies ran while one was open for 3% of the time, Pallas kernels for 0%

profile of v2, /device:TPU:1, one launch (start us, length us, event | category | flops | bytes accessed | tf_op | source)
XLA Modules:
  0.0 191.0 jit_solution(12010419521963558014)
XLA Ops:
  0.6 0.7 broadcast_in_dim.16
  1.3 0.8 reshape.85
  2.2 12.0 %all-to-all-start = ((f32[32,1,320]{2,1,0:T(1,128)}), f32[32,1,320]{2,1,0:T(1,128)S(1)}, u32[]{:S(2)}, u32[]{:S(2)}) async-start(f32[32,1,320]{2,1,0:T(1,128)} %reshape.85), calls=%async_computation | async-start | bytes 98304 | tf_op jit(solution)/shard_map/all_to_all | solution.py:181
  14.2 0.7 select_reduce_fusion
  15.0 0.7 broadcast_multiply_fusion.1
  15.6 1.0 copy.15
  16.6 0.1 convert_reduce_fusion.1
  16.7 0.7 broadcast_compare_fusion
  17.5 0.7 broadcast_multiply_fusion.weight
  18.2 2.1 %subtract_convert_fusion.obs = bf16[640,1024]{1,0:T(8,128)(2,1)S(1)} fusion(s32[640,1024]{1,0:T(8,128)} %param.9, f32[1024]{0:T(1024)S(1)} %broadcast_multiply_fusion.1), kind=kLoop, calls=%fused_computation | loop fusion | flops 1966080 | bytes 3936256 | tf_op jit(solution)/shard_map/convert_element_type | solution.py:203
  20.3 0.1 broadcast_compare_fusion.1
  20.4 2.5 %all-to-all-done = f32[32,1,320]{2,1,0:T(1,128)S(1)} async-done(((f32[32,1,320]{2,1,0:T(1,128)}), f32[32,1,320]{2,1,0:T(1,128)S(1)}, u32[]{:S(2)}, u32[]{:S(2)}) %all-to-all-start) | async-done | bytes 40992 | tf_op jit(solution)/shard_map/all_to_all | solution.py:181
  22.9 0.5 broadcast.55
  23.4 0.8 reduce
  24.2 0.2 reshape.86.mine
  24.4 2.1 %collective-permute-start = (f32[32,16,20]{2,1,0:T(8,128)S(1)}, f32[32,16,20]{2,1,0:T(8,128)S(1)}, u32[]{:S(2)}, u32[]{:S(2)}) collective-permute-start(f32[32,16,20]{2,1,0:T(8,128)S(1)} %reshape.86.mine), channel_id=1, source_target_pairs={{0,4},{4,0},{1,5},{5,1},{2,6},{6,2},{3,7},{7,3},{8,12},{12,8},{9,1... | collective-permute-start | bytes 122888 | tf_op jit(solution)/shard_map/ppermute | solution.py:146
  26.5 0.1 convert_reduce_fusion
  26.7 0.2 copy.17.miss
  26.8 0.8 collective-permute-done.other
  27.7 2.5 %shard_map.112 = (bf16[640,1024]{1,0:T(8,128)(2,1)S(1)}, f32[64,640]{1,0:T(8,128)S(1)}) custom-call(s32[1]{0:T(128)} %bitcast.place, bf16[640,1024]{1,0:T(8,128)(2,1)S(1)} %subtract_convert_fusion.obs, f32[640,4]{1,0:T(8,128)S(1)} %copy.17.miss, f32[640,20]{1,0:T(8,128)S(1)} %broadcast_multiply_fusion.weight, f32[32,16,20]{2,1,0:T(8,128)S(1)} %reshape.86.mine, ...), custom_call_target="tpu_custom_call" | custom-call | tf_op jit(solution)/shard_map/pallas_call | solution.py:228
  30.2 2.8 %collective-permute-start.3 = (f32[64,640]{1,0:T(8,128)S(1)}, f32[64,640]{1,0:T(8,128)S(1)}, u32[]{:S(2)}, u32[]{:S(2)}) collective-permute-start(f32[64,640]{1,0:T(8,128)S(1)} %get-tuple-element.23.own), channel_id=1, source_target_pairs={{0,3},{1,0},{2,1},{3,2},{4,7},{5,4},{6,5},{7,6},{8,11},{9,8},{10,9... | collective-permute-start | bytes 491528 | tf_op jit(solution)/shard_map/ppermute | solution.py:150
  33.0 0.3 collective-permute-start.2
  33.4 0.7 collective-permute-start.1
  34.1 5.5 %collective-permute-done.3.c = f32[64,640]{1,0:T(8,128)S(1)} collective-permute-done((f32[64,640]{1,0:T(8,128)S(1)}, f32[64,640]{1,0:T(8,128)S(1)}, u32[]{:S(2)}, u32[]{:S(2)}) %collective-permute-start.3) | collective-permute-done | bytes 163872 | tf_op jit(solution)/shard_map/ppermute | solution.py:150
  39.6 0.1 collective-permute-done.2.b
  39.7 4.5 %collective-permute-done.1.a = f32[64,640]{1,0:T(8,128)S(1)} collective-permute-done((f32[64,640]{1,0:T(8,128)S(1)}, f32[64,640]{1,0:T(8,128)S(1)}, u32[]{:S(2)}, u32[]{:S(2)}) %collective-permute-start.1) | collective-permute-done | bytes 163872 | tf_op jit(solution)/shard_map/ppermute | solution.py:150
  44.2 0.8 shard_map.113
  44.9 0.5 collective-permute-start.4
  45.4 1.2 collective-permute-done.4
  46.6 17.3 %all_to_all.35.parts = f32[32,16,128]{2,1,0:T(8,128)S(1)} all-to-all(f32[32,16,128]{2,1,0:T(8,128)S(1)} %add.37), channel_id=1, replica_groups=mesh['chip'=32,'core'=2,'snp'=4] {'chip'}, dimensions={0} | all-to-all | bytes 524288 | tf_op jit(solution)/shard_map/all_to_all | solution.py:156
  63.9 0.1 shard_map.114
  64.0 15.0 %all_to_all.36.mine = f32[32,16,128]{2,1,0:T(8,128)S(1)} all-to-all(f32[32,16,128]{2,1,0:T(8,128)S(1)} %shard_map.114), channel_id=1, replica_groups=mesh['chip'=32,'core'=2,'snp'=4] {'chip'}, dimensions={0} | all-to-all | bytes 524288 | tf_op jit(solution)/shard_map/all_to_all | solution.py:158
  79.0 3.3 %collective-permute-start.5 = (f32[32,16,128]{2,1,0:T(8,128)S(1)}, f32[32,16,128]{2,1,0:T(8,128)S(1)}, u32[]{:S(2)}, u32[]{:S(2)}) collective-permute-start(f32[32,16,128]{2,1,0:T(8,128)S(1)} %all_to_all.36.mine), channel_id=1, source_target_pairs={{0,4},{4,0},{1,5},{5,1},{2,6},{6,2},{3,7},{7,3},{8,12},{12,8},{9,1... | collective-permute-start | bytes 786440 | tf_op jit(solution)/shard_map/ppermute | solution.py:146
  82.2 1.2 collective-permute-done.5.other
  83.4 3.1 %shard_map.115 = (f32[64,1024]{1,0:T(8,128)S(1)}, f32[64,640]{1,0:T(8,128)S(1)}, f32[64,64]{1,0:T(8,128)S(1)}, bf16[64,832]{1,0:T(8,128)(2,1)S(1)}) custom-call(s32[1]{0:T(128)} %bitcast.place, f32[32,16,128]{2,1,0:T(8,128)S(1)} %all_to_all.36.mine, f32[32,16,128]{2,1,0:T(8,128)S(1)} %collective-permute-done.5.other, bf16[640,1024]{1,0:T(8,128)(2,1)S(1)} %get-tuple-element.24.x), custom_call_target="tpu_custom_call" | custom-call | tf_op jit(solution)/shard_map/pallas_call | solution.py:228
  86.5 0.4 collective-permute-start.8
  86.9 0.3 collective-permute-start.7
  87.2 0.8 collective-permute-start.6
  88.0 2.9 %collective-permute-done.8.c = bf16[64,832]{1,0:T(8,128)(2,1)S(1)} collective-permute-done((bf16[64,832]{1,0:T(8,128)(2,1)S(1)}, bf16[64,832]{1,0:T(8,128)(2,1)S(1)}, u32[]{:S(2)}, u32[]{:S(2)}) %collective-permute-start.8) | collective-permute-done | bytes 106528 | tf_op jit(solution)/shard_map/ppermute | solution.py:150
  90.9 1.5 collective-permute-done.7.b
  92.4 3.5 %collective-permute-done.6.a = bf16[64,832]{1,0:T(8,128)(2,1)S(1)} collective-permute-done((bf16[64,832]{1,0:T(8,128)(2,1)S(1)}, bf16[64,832]{1,0:T(8,128)(2,1)S(1)}, u32[]{:S(2)}, u32[]{:S(2)}) %collective-permute-start.6) | collective-permute-done | bytes 106528 | tf_op jit(solution)/shard_map/ppermute | solution.py:150
  95.9 3.5 %shard_map.116 = (f32[64,640]{1,0:T(8,128)}, f32[64,1024]{1,0:T(8,128)}, f32[32,16,128]{2,1,0:T(8,128)S(1)}, f32[32,16,128]{2,1,0:T(8,128)S(1)}) custom-call(s32[1]{0:T(128)} %bitcast.place, f32[64,640]{1,0:T(8,128)S(1)} %get-tuple-element.27.product, f32[64,64]{1,0:T(8,128)S(1)} %get-tuple-element.28.gram, bf16[64,832]{1,0:T(8,128)(2,1)S(1)} %collective-permute-done.6.a, ...), custom_call_target="tpu_custom_call" | custom-call | tf_op jit(solution)/shard_map/pallas_call | solution.py:228
  99.4 0.5 collective-permute-start.9
  99.9 1.2 collective-permute-done.9
  101.1 14.9 %all_to_all.37.parts = f32[32,16,128]{2,1,0:T(8,128)S(1)} all-to-all(f32[32,16,128]{2,1,0:T(8,128)S(1)} %add.38), channel_id=1, replica_groups=mesh['chip'=32,'core'=2,'snp'=4] {'chip'}, dimensions={0} | all-to-all | bytes 524288 | tf_op jit(solution)/shard_map/all_to_all | solution.py:156
  116.0 0.1 shard_map.117
  116.0 15.0 %all_to_all.38.mine = f32[32,16,128]{2,1,0:T(8,128)S(1)} all-to-all(f32[32,16,128]{2,1,0:T(8,128)S(1)} %shard_map.117), channel_id=1, replica_groups=mesh['chip'=32,'core'=2,'snp'=4] {'chip'}, dimensions={0} | all-to-all | bytes 524288 | tf_op jit(solution)/shard_map/all_to_all | solution.py:158
  131.1 3.3 %collective-permute-start.10 = (f32[32,16,128]{2,1,0:T(8,128)S(1)}, f32[32,16,128]{2,1,0:T(8,128)S(1)}, u32[]{:S(2)}, u32[]{:S(2)}) collective-permute-start(f32[32,16,128]{2,1,0:T(8,128)S(1)} %all_to_all.38.mine), channel_id=1, source_target_pairs={{0,4},{4,0},{1,5},{5,1},{2,6},{6,2},{3,7},{7,3},{8,12},{12,8},{9,1... | collective-permute-start | bytes 786440 | tf_op jit(solution)/shard_map/ppermute | solution.py:146
  134.3 1.2 collective-permute-done.10.other
  135.5 3.1 %shard_map.118 = (f32[64,1024]{1,0:T(8,128)S(1)}, f32[64,640]{1,0:T(8,128)S(1)}, f32[64,64]{1,0:T(8,128)S(1)}, bf16[64,832]{1,0:T(8,128)(2,1)S(1)}) custom-call(s32[1]{0:T(128)} %bitcast.place, f32[32,16,128]{2,1,0:T(8,128)S(1)} %all_to_all.38.mine, f32[32,16,128]{2,1,0:T(8,128)S(1)} %collective-permute-done.10.other, bf16[640,1024]{1,0:T(8,128)(2,1)S(1)} %get-tuple-element.24.x), custom_call_target="tpu_custom_call" | custom-call | tf_op jit(solution)/shard_map/pallas_call | solution.py:228
  138.6 0.6 collective-permute-start.13
  139.2 0.9 collective-permute-start.11
  140.1 2.9 %collective-permute-done.13.c = bf16[64,832]{1,0:T(8,128)(2,1)S(1)} collective-permute-done((bf16[64,832]{1,0:T(8,128)(2,1)S(1)}, bf16[64,832]{1,0:T(8,128)(2,1)S(1)}, u32[]{:S(2)}, u32[]{:S(2)}) %collective-permute-start.13) | collective-permute-done | bytes 106528 | tf_op jit(solution)/shard_map/ppermute | solution.py:150
  143.0 1.8 collective-permute-done.12.b
  144.7 3.5 %collective-permute-done.11.a = bf16[64,832]{1,0:T(8,128)(2,1)S(1)} collective-permute-done((bf16[64,832]{1,0:T(8,128)(2,1)S(1)}, bf16[64,832]{1,0:T(8,128)(2,1)S(1)}, u32[]{:S(2)}, u32[]{:S(2)}) %collective-permute-start.11) | collective-permute-done | bytes 106528 | tf_op jit(solution)/shard_map/ppermute | solution.py:150
  148.2 3.4 %shard_map.119 = (f32[64,640]{1,0:T(8,128)S(1)}, f32[64,1024]{1,0:T(8,128)}, f32[32,16,128]{2,1,0:T(8,128)S(1)}, f32[32,16,128]{2,1,0:T(8,128)S(1)}) custom-call(s32[1]{0:T(128)} %bitcast.place, f32[64,640]{1,0:T(8,128)S(1)} %get-tuple-element.33.product, f32[64,64]{1,0:T(8,128)S(1)} %get-tuple-element.34.gram, ...), custom_call_target="tpu_custom_call" | custom-call | tf_op jit(solution)/shard_map/pallas_call | solution.py:228
  151.6 0.5 collective-permute-start.14
  152.1 1.2 collective-permute-done.14
  153.3 14.9 %all_to_all.39.parts = f32[32,16,128]{2,1,0:T(8,128)S(1)} all-to-all(f32[32,16,128]{2,1,0:T(8,128)S(1)} %add.39), channel_id=1, replica_groups=mesh['chip'=32,'core'=2,'snp'=4] {'chip'}, dimensions={0} | all-to-all | bytes 524288 | tf_op jit(solution)/shard_map/all_to_all | solution.py:156
  168.3 0.1 shard_map.120
  168.3 15.0 %all_to_all.40.mine = f32[32,16,128]{2,1,0:T(8,128)S(1)} all-to-all(f32[32,16,128]{2,1,0:T(8,128)S(1)} %shard_map.120), channel_id=1, replica_groups=mesh['chip'=32,'core'=2,'snp'=4] {'chip'}, dimensions={0} | all-to-all | bytes 524288 | tf_op jit(solution)/shard_map/all_to_all | solution.py:158
  183.3 3.3 %collective-permute-start.15 = (f32[32,16,128]{2,1,0:T(8,128)S(1)}, f32[32,16,128]{2,1,0:T(8,128)S(1)}, u32[]{:S(2)}, u32[]{:S(2)}) collective-permute-start(f32[32,16,128]{2,1,0:T(8,128)S(1)} %all_to_all.40.mine), channel_id=1, source_target_pairs={{0,4},{4,0},{1,5},{5,1},{2,6},{6,2},{3,7},{7,3},{8,12},{12,8},{9,1... | collective-permute-start | bytes 786440 | tf_op jit(solution)/shard_map/ppermute | solution.py:146
  186.6 1.2 collective-permute-done.15.other
  187.8 3.2 %shard_map.121 = (f32[64,640]{1,0:T(8,128)}, f32[64,1024]{1,0:T(8,128)}) custom-call(s32[1]{0:T(128)} %bitcast.place, f32[32,16,128]{2,1,0:T(8,128)S(1)} %all_to_all.40.mine, f32[32,16,128]{2,1,0:T(8,128)S(1)} %collective-permute-done.15.other, f32[64,640]{1,0:T(8,128)S(1)} %get-tuple-element.39.samples), custom_call_target="tpu_custom_call" | custom-call | tf_op jit(solution)/shard_map/pallas_call | solution.py:228
  (10 shorter events, 0.1 us)
Async XLA Ops:
  2.2 18.1 %copy-start.1 = (s32[48]{0:T(128)S(1)}, s32[48]{0:T(128)}, u32[]{:S(2)}) copy-start(s32[48]{0:T(128)} %param.17) | copy-start | bytes 580
  2.2 20.7 %all-to-all-start = ((f32[32,1,320]{2,1,0:T(1,128)}), f32[32,1,320]{2,1,0:T(1,128)S(1)}, u32[]{:S(2)}, u32[]{:S(2)}) async-start(f32[32,1,320]{2,1,0:T(1,128)} %reshape.85), calls=%async_computation | async-start | bytes 98304 | tf_op jit(solution)/shard_map/all_to_all | solution.py:181
  17.5 10.2 %copy-start = (bf16[1024,64]{0,1:T(8,128)(2,1)S(1)}, bf16[1024,64]{0,1:T(8,128)(2,1)}, u32[]{:S(2)}) copy-start(bf16[1024,64]{0,1:T(8,128)(2,1)} %param.14) | copy-start | bytes 393220
  24.4 3.3 %collective-permute-start = (f32[32,16,20]{2,1,0:T(8,128)S(1)}, f32[32,16,20]{2,1,0:T(8,128)S(1)}, u32[]{:S(2)}, u32[]{:S(2)}) collective-permute-start(f32[32,16,20]{2,1,0:T(8,128)S(1)} %reshape.86.mine), channel_id=1, source_target_pairs={{0,4},{4,0},{1,5},{5,1},{2,6},{6,2},{3,7},{7,3},{8,12},{12,8},{9,1... | collective-permute-start | bytes 122888 | tf_op jit(solution)/shard_map/ppermute | solution.py:146
  30.2 9.4 %collective-permute-start.3 = (f32[64,640]{1,0:T(8,128)S(1)}, f32[64,640]{1,0:T(8,128)S(1)}, u32[]{:S(2)}, u32[]{:S(2)}) collective-permute-start(f32[64,640]{1,0:T(8,128)S(1)} %get-tuple-element.23.own), channel_id=1, source_target_pairs={{0,3},{1,0},{2,1},{3,2},{4,7},{5,4},{6,5},{7,6},{8,11},{9,8},{10,9... | collective-permute-start | bytes 491528 | tf_op jit(solution)/shard_map/ppermute | solution.py:150
  33.0 6.6 %collective-permute-start.2 = (f32[64,640]{1,0:T(8,128)S(1)}, f32[64,640]{1,0:T(8,128)S(1)}, u32[]{:S(2)}, u32[]{:S(2)}) collective-permute-start(f32[64,640]{1,0:T(8,128)S(1)} %get-tuple-element.23.own), channel_id=1, source_target_pairs={{0,2},{1,3},{2,0},{3,1},{4,6},{5,7},{6,4},{7,5},{8,10},{9,11},{10,... | collective-permute-start | bytes 491528 | tf_op jit(solution)/shard_map/ppermute | solution.py:150
  33.4 10.8 %collective-permute-start.1 = (f32[64,640]{1,0:T(8,128)S(1)}, f32[64,640]{1,0:T(8,128)S(1)}, u32[]{:S(2)}, u32[]{:S(2)}) collective-permute-start(f32[64,640]{1,0:T(8,128)S(1)} %get-tuple-element.23.own), channel_id=1, source_target_pairs={{0,1},{1,2},{2,3},{3,0},{4,5},{5,6},{6,7},{7,4},{8,9},{9,10},{10,1... | collective-permute-start | bytes 491528 | tf_op jit(solution)/shard_map/ppermute | solution.py:150
  44.9 1.7 collective-permute-start.4
  79.0 4.5 %collective-permute-start.5 = (f32[32,16,128]{2,1,0:T(8,128)S(1)}, f32[32,16,128]{2,1,0:T(8,128)S(1)}, u32[]{:S(2)}, u32[]{:S(2)}) collective-permute-start(f32[32,16,128]{2,1,0:T(8,128)S(1)} %all_to_all.36.mine), channel_id=1, source_target_pairs={{0,4},{4,0},{1,5},{5,1},{2,6},{6,2},{3,7},{7,3},{8,12},{12,8},{9,1... | collective-permute-start | bytes 786440 | tf_op jit(solution)/shard_map/ppermute | solution.py:146
  86.5 4.4 %collective-permute-start.8 = (bf16[64,832]{1,0:T(8,128)(2,1)S(1)}, bf16[64,832]{1,0:T(8,128)(2,1)S(1)}, u32[]{:S(2)}, u32[]{:S(2)}) collective-permute-start(bf16[64,832]{1,0:T(8,128)(2,1)S(1)} %get-tuple-element.29), channel_id=1, source_target_pairs={{0,3},{1,0},{2,1},{3,2},{4,7},{5,4},{6,5},{7,6},{8,11},{9,8},{10,9... | collective-permute-start | bytes 319496 | tf_op jit(solution)/shard_map/ppermute | solution.py:150
  86.9 5.6 %collective-permute-start.7 = (bf16[64,832]{1,0:T(8,128)(2,1)S(1)}, bf16[64,832]{1,0:T(8,128)(2,1)S(1)}, u32[]{:S(2)}, u32[]{:S(2)}) collective-permute-start(bf16[64,832]{1,0:T(8,128)(2,1)S(1)} %get-tuple-element.29), channel_id=1, source_target_pairs={{0,2},{1,3},{2,0},{3,1},{4,6},{5,7},{6,4},{7,5},{8,10},{9,11},{10,... | collective-permute-start | bytes 319496 | tf_op jit(solution)/shard_map/ppermute | solution.py:150
  87.2 8.7 %collective-permute-start.6 = (bf16[64,832]{1,0:T(8,128)(2,1)S(1)}, bf16[64,832]{1,0:T(8,128)(2,1)S(1)}, u32[]{:S(2)}, u32[]{:S(2)}) collective-permute-start(bf16[64,832]{1,0:T(8,128)(2,1)S(1)} %get-tuple-element.29), channel_id=1, source_target_pairs={{0,1},{1,2},{2,3},{3,0},{4,5},{5,6},{6,7},{7,4},{8,9},{9,10},{10,1... | collective-permute-start | bytes 319496 | tf_op jit(solution)/shard_map/ppermute | solution.py:150
  99.4 1.6 collective-permute-start.9
  131.1 4.5 %collective-permute-start.10 = (f32[32,16,128]{2,1,0:T(8,128)S(1)}, f32[32,16,128]{2,1,0:T(8,128)S(1)}, u32[]{:S(2)}, u32[]{:S(2)}) collective-permute-start(f32[32,16,128]{2,1,0:T(8,128)S(1)} %all_to_all.38.mine), channel_id=1, source_target_pairs={{0,4},{4,0},{1,5},{5,1},{2,6},{6,2},{3,7},{7,3},{8,12},{12,8},{9,1... | collective-permute-start | bytes 786440 | tf_op jit(solution)/shard_map/ppermute | solution.py:146
  138.6 4.4 %collective-permute-start.13 = (bf16[64,832]{1,0:T(8,128)(2,1)S(1)}, bf16[64,832]{1,0:T(8,128)(2,1)S(1)}, u32[]{:S(2)}, u32[]{:S(2)}) collective-permute-start(bf16[64,832]{1,0:T(8,128)(2,1)S(1)} %get-tuple-element.35), channel_id=1, source_target_pairs={{0,3},{1,0},{2,1},{3,2},{4,7},{5,4},{6,5},{7,6},{8,11},{9,8},{10,9... | collective-permute-start | bytes 319496 | tf_op jit(solution)/shard_map/ppermute | solution.py:150
  139.2 5.5 %collective-permute-start.12 = (bf16[64,832]{1,0:T(8,128)(2,1)S(1)}, bf16[64,832]{1,0:T(8,128)(2,1)S(1)}, u32[]{:S(2)}, u32[]{:S(2)}) collective-permute-start(bf16[64,832]{1,0:T(8,128)(2,1)S(1)} %get-tuple-element.35), channel_id=1, source_target_pairs={{0,2},{1,3},{2,0},{3,1},{4,6},{5,7},{6,4},{7,5},{8,10},{9,11},{10,... | collective-permute-start | bytes 319496 | tf_op jit(solution)/shard_map/ppermute | solution.py:150
  139.2 9.0 %collective-permute-start.11 = (bf16[64,832]{1,0:T(8,128)(2,1)S(1)}, bf16[64,832]{1,0:T(8,128)(2,1)S(1)}, u32[]{:S(2)}, u32[]{:S(2)}) collective-permute-start(bf16[64,832]{1,0:T(8,128)(2,1)S(1)} %get-tuple-element.35), channel_id=1, source_target_pairs={{0,1},{1,2},{2,3},{3,0},{4,5},{5,6},{6,7},{7,4},{8,9},{9,10},{10,1... | collective-permute-start | bytes 319496 | tf_op jit(solution)/shard_map/ppermute | solution.py:150
  151.6 1.7 collective-permute-start.14
  183.3 4.5 %collective-permute-start.15 = (f32[32,16,128]{2,1,0:T(8,128)S(1)}, f32[32,16,128]{2,1,0:T(8,128)S(1)}, u32[]{:S(2)}, u32[]{:S(2)}) collective-permute-start(f32[32,16,128]{2,1,0:T(8,128)S(1)} %all_to_all.40.mine), channel_id=1, source_target_pairs={{0,4},{4,0},{1,5},{5,1},{2,6},{6,2},{3,7},{7,3},{8,12},{12,8},{9,1... | collective-permute-start | bytes 786440 | tf_op jit(solution)/shard_map/ppermute | solution.py:146

commit v3 on v2

--- a/solution.py
+++ b/solution.py
@@ -13,6 +13,7 @@
 BLOCKS = 16
 LANES = 128
 SUB = 8
+GROUP = 32
 F32 = jnp.float32
 BF16 = jnp.bfloat16
 HIGH = lax.Precision.HIGHEST
@@ -179,47 +180,71 @@
         samp_index = lax.axis_index("chip") * 2 + core
 
         right_mine = lax.all_to_all(
-            jnp.broadcast_to(right_factors[None], (chips, *right_factors.shape)), "chip", 0, 0
+            jnp.broadcast_to(
+                jnp.pad(right_factors, ((0, 0), (0, LANES - rank)))[None],
+                (chips, right_factors.shape[0], LANES),
+            ),
+            "chip",
+            0,
+            0,
         )
         right_other = swap(right_mine)
 
         batch_range = jnp.arange(BATCHES, dtype=jnp.int32)
         local_blocks = col_width // BLOCK
-        block_range = lax.axis_index("snp") * local_blocks + jnp.arange(
-            local_blocks, dtype=jnp.int32
-        )
+        snp_index = lax.axis_index("snp")
         ends = jnp.sum(
             jnp.where(batch_range[:, None] <= batch_range[None, :], batch_sizes[:, None], 0), axis=0
         )
         row_ids = samp_index * row_count + jnp.arange(row_count, dtype=jnp.int32)
         batch_of = jnp.sum((row_ids[:, None] >= ends[None, :]).astype(jnp.int32), axis=1)
-        missing = jnp.sum(
+        away = jnp.arange(BLOCKS, dtype=jnp.int32)
+        block_ids = (snp_index - away // local_blocks) % snp * local_blocks + away % local_blocks
+        missing_rows = jnp.sum(
             (
-                (batch_of[:, None, None] == missing_batch[None, None, :])
-                & (block_range[None, :, None] == missing_block[None, None, :])
+                (batch_of[None, :, None] == missing_batch[None, None, :])
+                & (block_ids[:, None, None] == missing_block[None, None, :])
             ).astype(F32),
             axis=2,
         )
-        observed = (genotype.astype(F32) - 2.0 * freqs[None, :]).astype(BF16)
+        missing = missing_rows[:local_blocks].T
         weighted = left_factors * singular[None, :]
-
-        def build_kernel(place, obs, miss, weight, mine, other, omega, x_out, start):
-            first = place[0] == 0
-            r_mine, r_other = mine[...], other[...]
-            low = jnp.where(first, r_mine, r_other)
-            high = jnp.where(first, r_other, r_mine)
-            right = jnp.stack([low, high], axis=1).reshape(col_width, rank)
-            lowrank = exact_dot(weight[...], right, 1, 1)
-            pieces = []
-            for j in range(local_blocks):
-                at = slice(BLOCK * j, BLOCK * (j + 1))
-                gone = jnp.broadcast_to(miss[:, j : j + 1], (row_count, BLOCK)) > 0.5
-                pieces.append(jnp.where(gone, lowrank[:, at], obs[:, at].astype(F32)))
-            x = jnp.concatenate(pieces, axis=1).astype(BF16)
-            x_out[...] = x
+        weight_rows = jnp.pad(weighted.T, ((0, GROUP - rank), (0, 0)))
+        weight_lanes = jnp.pad(weighted, ((0, 0), (0, LANES - rank)))
+        omega = sketch.T
+
+        def gone_blocks(miss, rows):
+            return [
+                jnp.broadcast_to(miss[:, j : j + 1], (rows, BLOCK)) > 0.5
+                for j in range(local_blocks)
+            ]
+
+        def observe_kernel(geno, freq, miss, om, obs, start):
+            rows = geno.shape[0]
+            values = geno[...].astype(F32) - 2.0 * freq[...]
+            gone = jnp.concatenate(gone_blocks(miss, rows), axis=1)
+            kept = jnp.where(gone, 0.0, values).astype(BF16)
+            obs[...] = kept
             start[...] = lax.dot_general(
-                omega[...], x, (((1,), (1,)), ((), ())), preferred_element_type=F32
+                om[...], kept, (((1,), (1,)), ((), ())), preferred_element_type=F32
             )
+
+        observed, start = pl.pallas_call(
+            observe_kernel,
+            grid=(row_count // LANES,),
+            out_shape=(shape_of((row_count, col_width), BF16), shape_of((width, row_count))),
+            in_specs=[
+                pl.BlockSpec((LANES, col_width), lambda i: (i, 0)),
+                pl.BlockSpec((1, col_width), lambda i: (0, 0)),
+                pl.BlockSpec((LANES, local_blocks), lambda i: (i, 0)),
+                pl.BlockSpec((width, col_width), lambda i: (0, 0)),
+            ],
+            out_specs=(
+                pl.BlockSpec((LANES, col_width), lambda i: (i, 0)),
+                pl.BlockSpec((width, LANES), lambda i: (0, i)),
+            ),
+        )(genotype, freqs.reshape(1, col_width), missing, omega)
+        start_others = snp_others(start)
 
         def call_with_place(body, outs, *operands):
             specs = [pl.BlockSpec(memory_space=pltpu.SMEM)] + [
@@ -232,22 +257,64 @@
                 compiler_params=pltpu.CompilerParams(vmem_limit_bytes=48 * 1024 * 1024),
             )(place, *operands)
 
-        matrix, start = call_with_place(
+        def right_rows(place, mine, other):
+            first = place[0] == 0
+            r_mine, r_other = mine[...], other[...]
+            low = jnp.where(first, r_mine, r_other)
+            high = jnp.where(first, r_other, r_mine)
+            return jnp.stack([low, high], axis=1).reshape(col_width, LANES)
+
+        def mix_kernel(place, mine, other, om, mixed):
+            right = right_rows(place, mine, other)
+            pieces = [
+                exact_dot(
+                    om[:, BLOCK * j : BLOCK * (j + 1)].astype(F32),
+                    right[BLOCK * j : BLOCK * (j + 1)],
+                    1,
+                    0,
+                )[:, :GROUP]
+                for j in range(local_blocks)
+            ]
+            mixed[...] = jnp.concatenate(pieces, axis=1)
+
+        def build_kernel(place, obs, miss, weight, mine, other, x_out):
+            right = right_rows(place, mine, other)
+            for j, gone in enumerate(gone_blocks(miss, row_count)):
+                at = slice(BLOCK * j, BLOCK * (j + 1))
+                lowrank = exact_dot(weight[...], right[at], 1, 1)
+                x_out[:, at] = jnp.where(gone, lowrank.astype(BF16), obs[:, at])
+
+        mixed = call_with_place(
+            mix_kernel,
+            shape_of((width, local_blocks * GROUP)),
+            right_mine,
+            right_other,
+            omega,
+        )
+        mixed_others = snp_others(mixed)
+        matrix = call_with_place(
             build_kernel,
-            (shape_of((row_count, col_width), BF16), shape_of((width, row_count))),
+            shape_of((row_count, col_width), BF16),
             observed,
             missing,
-            weighted,
+            weight_lanes,
             right_mine,
             right_other,
-            sketch.T,
         )
 
         part_shape = shape_of((chips, 2 * SUB, LANES))
         packed = row_count + 3 * width
 
-        def first_kernel(place, own, a, b, c, x, samples_out, mine, other):
+        def first_kernel(
+            place, own, a, b, c, q0, q1, q2, q3, miss, weight, x, samples_out, mine, other
+        ):
             samples = own[...] + a[...] + b[...] + c[...]
+            for k, q in enumerate((q0, q1, q2, q3)):
+                masked = [
+                    weight[...] * miss[local_blocks * k + j : local_blocks * k + j + 1, :]
+                    for j in range(local_blocks)
+                ]
+                samples = samples + exact_dot(q[...], jnp.concatenate(masked, axis=0), 1, 0)
             samples_out[...] = samples
             write_send(
                 split_dot(samples, x[...], 0),
@@ -302,7 +369,11 @@
             first_kernel,
             (samples_shape, part_shape, part_shape),
             start,
-            *snp_others(start),
+            *start_others,
+            mixed,
+            *mixed_others,
+            missing_rows,
+            weight_rows,
             matrix,
         )
         columns = None

time: 192 us -> 195 us (1.016)
  starting transfers between devices: 32.4 us -> 45.5 us
  waiting for transfers between devices: 36.5 us -> 26.5 us
  Pallas kernels: 19.7 us -> 25.8 us
  other arithmetic: 6.15 us -> 2.97 us
  blocking collectives: 92.1 us -> 90.1 us
    ppermute x9 -> x12, waiting for transfers between devices: 26.1 us -> 10.7 us  [snp_others(): lax.ppermute(value, 'snp', [(i, (i + k) % snp) for i in range(snp)])]
    ppermute x9 -> x12, starting transfers between devices: 6.89 us -> 16.6 us  [snp_others(): lax.ppermute(value, 'snp', [(i, (i + k) % snp) for i in range(snp)])]
    all_to_all x1, waiting for transfers between devices: 2.52 us -> 8.8 us  [on_device(): lax.all_to_all(jnp.broadcast_to(jnp.pad(right_factors, ((0, 0), (0, LANES...]
    pallas_call x0 -> x1, Pallas kernels: none -> 4.87 us  [on_device(): pl.pallas_call(observe_kernel, grid=(row_count // LANES,), out_shape=(sha...]
    ppermute x7, starting transfers between devices: 13.5 us -> 16.9 us  [swap(): return lax.ppermute(value, 'core', [(0, 1), (1, 0)])]
    convert_element_type x1 -> x0, other arithmetic: 2.09 us -> none  [on_device(): observed = (genotype.astype(F32) - 2.0 * freqs[None, :]).astype(BF16)]
    all_to_all x3, blocking collectives: 47.1 us -> 45.1 us  [samp_sum(): got = lax.all_to_all(send, 'chip', 0, 0)]
    pallas_call x7 -> x8, Pallas kernels: 19.5 us -> 20.7 us  [call_with_place(): pl.pallas_call(body, out_shape=outs, in_specs=specs, compiler_params=pltp...]
  transfers between devices with their start and end apart: 17 -> 20, of which waited for: 17 -> 16; matrix products, arithmetic and copies ran while one was open for 3% -> 2% of each run, Pallas kernels for 0% -> 4%
where the time goes in v3:
time: 195 us; the launch traced here: 194 us
  blocking collectives  90.1 us (46%)
  starting transfers between devices  45.5 us (23%)
  waiting for transfers between devices  26.5 us (14%)
  Pallas kernels  25.8 us (13%)
  other arithmetic  2.97 us (2%)
  local copies, waits for them, and re-layouts  2.57 us (1%)
    all_to_all x3, blocking collectives, samp_sum(): got = lax.all_to_all(send, 'chip', 0, 0)  45.1 us
    all_to_all x3, blocking collectives, samp_sum(): whole = lax.all_to_all(spread, 'chip', 0, 0)  45 us
    pallas_call x8, Pallas kernels, call_with_place(): pl.pallas_call(body, out_shape=outs, in_specs=specs, compiler_params=pltp...  20.7 us
    ppermute x7, starting transfers between devices, swap(): return lax.ppermute(value, 'core', [(0, 1), (1, 0)])  16.9 us
    ppermute x12, starting transfers between devices, snp_others(): lax.ppermute(value, 'snp', [(i, (i + k) % snp) for i in range(snp)])  16.6 us
    all_to_all x1, starting transfers between devices, on_device(): lax.all_to_all(jnp.broadcast_to(jnp.pad(right_factors, ((0, 0), (0, LANES...  12 us
    ppermute x12, waiting for transfers between devices, snp_others(): lax.ppermute(value, 'snp', [(i, (i + k) % snp) for i in range(snp)])  10.7 us
    all_to_all x1, waiting for transfers between devices, on_device(): lax.all_to_all(jnp.broadcast_to(jnp.pad(right_factors, ((0, 0), (0, LANES...  8.8 us
  transfers between devices with their start and end apart: 20, of which 16 were waited for; matrix products, arithmetic and copies ran while one was open for 2% of the time, Pallas kernels for 4%

profile of v3, /device:TPU:1, one launch (start us, length us, event | category | flops | bytes accessed | tf_op | source)
XLA Modules:
  0.0 194.2 jit_solution(453766181278688629)
XLA Ops:
  0.6 0.7 pad.12
  1.3 0.7 broadcast_in_dim.16
  2.1 12.0 %all-to-all-start = ((f32[32,16,128]{2,1,0:T(8,128)}), f32[32,16,128]{2,1,0:T(8,128)S(1)}, u32[]{:S(2)}, u32[]{:S(2)}) async-start(f32[32,16,128]{2,1,0:T(8,128)} %broadcast_in_dim.16), calls=%async_computation | async-start | bytes 524288 | tf_op jit(solution)/shard_map/all_to_all | solution.py:182
  14.1 0.8 select_reduce_fusion
  14.9 0.1 convert_reduce_fusion.1
  15.0 0.7 broadcast_compare_fusion.1
  15.7 0.7 broadcast_compare_fusion
  16.5 8.8 %all-to-all-done.mine = f32[32,16,128]{2,1,0:T(8,128)S(1)} async-done(((f32[32,16,128]{2,1,0:T(8,128)}), f32[32,16,128]{2,1,0:T(8,128)S(1)}, u32[]{:S(2)}, u32[]{:S(2)}) %all-to-all-start) | async-done | bytes 262176 | tf_op jit(solution)/shard_map/all_to_all | solution.py:182
  25.3 2.5 %collective-permute-start.3 = (f32[32,16,128]{2,1,0:T(8,128)S(1)}, f32[32,16,128]{2,1,0:T(8,128)S(1)}, u32[]{:S(2)}, u32[]{:S(2)}) collective-permute-start(f32[32,16,128]{2,1,0:T(8,128)S(1)} %all-to-all-done.mine), channel_id=1, source_target_pairs={{0,4},{4,0},{1,5},{5,1},{2,6},{6,2},{3,7},{7,3},{8,12},{12,8},{9,1... | collective-permute-start | bytes 786440 | tf_op jit(solution)/shard_map/ppermute | solution.py:147
  27.7 0.4 convert_reduce_fusion.miss
  28.1 0.9 copy.15
  29.0 4.9 %shard_map.112 = (bf16[640,1024]{1,0:T(8,128)(2,1)}, f32[64,640]{1,0:T(8,128)}) custom-call(s32[640,1024]{1,0:T(8,128)} %geno.1, f32[1,1024]{1,0:T(1,128)} %bitcast.13, f32[640,4]{1,0:T(8,128)} %bitcast.9, bf16[64,1024]{1,0:T(8,128)(2,1)} %bitcast.11), custom_call_target="tpu_custom_call" | custom-call | tf_op jit(solution)/shard_map/pallas_call | solution.py:232
  33.9 1.3 collective-permute-start
  35.2 2.6 %collective-permute-start.1 = (f32[64,640]{1,0:T(8,128)}, f32[64,640]{1,0:T(8,128)S(1)}, u32[]{:S(2)}, u32[]{:S(2)}) collective-permute-start(f32[64,640]{1,0:T(8,128)} %get-tuple-element.23.own), channel_id=1, source_target_pairs={{0,2},{1,3},{2,0},{3,1},{4,6},{5,7},{6,4},{7,5},{8,10},{9,11},{10,... | collective-permute-start | bytes 491528 | tf_op jit(solution)/shard_map/ppermute | solution.py:151
  37.8 1.1 collective-permute-start.2
  38.9 0.1 broadcast_multiply_fusion
  39.0 0.5 shard_map.113.q0
  39.5 0.5 collective-permute-start.4
  39.9 0.8 collective-permute-start.5
  40.7 0.6 collective-permute-done.a
  41.3 1.4 collective-permute-start.6
  42.7 0.1 fusion.4
  42.8 0.2 copy.17
  43.0 2.3 %shard_map.114.x = bf16[640,1024]{1,0:T(8,128)(2,1)S(1)} custom-call(s32[1]{0:T(128)} %bitcast.place, bf16[640,1024]{1,0:T(8,128)(2,1)S(1)} %copy-done.1, f32[640,4]{1,0:T(8,128)S(1)} %bitcast.10, f32[640,128]{1,0:T(8,128)S(1)} %pad.14.clone.weight, f32[32,16,128]{2,1,0:T(8,128)S(1)} %all-to-all-done.mine, f32[32,16,128]{2,1,0:T(8,128)S(1)} %collective-permute-done.3.other), custom_call_target="tpu_custom_call" | custom-call | tf_op jit(solution)/shard_map/pallas_call | solution.py:253
  45.3 0.7 collective-permute-done.1.b
  46.0 1.2 collective-permute-done.4.q1
  47.2 1.8 shard_map.115
  48.9 1.0 collective-permute-start.7
  49.9 1.2 collective-permute-done.7
  51.1 15.2 %all_to_all.35.parts = f32[32,16,128]{2,1,0:T(8,128)S(1)} all-to-all(f32[32,16,128]{2,1,0:T(8,128)S(1)} %add.64), channel_id=1, replica_groups=mesh['chip'=32,'core'=2,'snp'=4] {'chip'}, dimensions={0} | all-to-all | bytes 524288 | tf_op jit(solution)/shard_map/all_to_all | solution.py:157
  66.3 0.1 shard_map.116
  66.4 15.0 %all_to_all.36.mine = f32[32,16,128]{2,1,0:T(8,128)S(1)} all-to-all(f32[32,16,128]{2,1,0:T(8,128)S(1)} %shard_map.116), channel_id=1, replica_groups=mesh['chip'=32,'core'=2,'snp'=4] {'chip'}, dimensions={0} | all-to-all | bytes 524288 | tf_op jit(solution)/shard_map/all_to_all | solution.py:159
  81.4 3.3 %collective-permute-start.8 = (f32[32,16,128]{2,1,0:T(8,128)S(1)}, f32[32,16,128]{2,1,0:T(8,128)S(1)}, u32[]{:S(2)}, u32[]{:S(2)}) collective-permute-start(f32[32,16,128]{2,1,0:T(8,128)S(1)} %all_to_all.36.mine), channel_id=1, source_target_pairs={{0,4},{4,0},{1,5},{5,1},{2,6},{6,2},{3,7},{7,3},{8,12},{12,8},{9,1... | collective-permute-start | bytes 786440 | tf_op jit(solution)/shard_map/ppermute | solution.py:147
  84.7 1.2 collective-permute-done.8.other
  85.8 3.1 %shard_map.117 = (f32[64,1024]{1,0:T(8,128)S(1)}, f32[64,640]{1,0:T(8,128)S(1)}, f32[64,64]{1,0:T(8,128)S(1)}, bf16[64,832]{1,0:T(8,128)(2,1)S(1)}) custom-call(s32[1]{0:T(128)} %bitcast.place, f32[32,16,128]{2,1,0:T(8,128)S(1)} %all_to_all.36.mine, f32[32,16,128]{2,1,0:T(8,128)S(1)} %collective-permute-done.8.other, bf16[640,1024]{1,0:T(8,128)(2,1)S(1)} %shard_map.114.x), custom_call_target="tpu_custom_call" | custom-call | tf_op jit(solution)/shard_map/pallas_call | solution.py:253
  88.9 3.4 %collective-permute-start.10 = (bf16[64,832]{1,0:T(8,128)(2,1)S(1)}, bf16[64,832]{1,0:T(8,128)(2,1)S(1)}, u32[]{:S(2)}, u32[]{:S(2)}) collective-permute-start(bf16[64,832]{1,0:T(8,128)(2,1)S(1)} %get-tuple-element.29), channel_id=1, source_target_pairs={{0,2},{1,3},{2,0},{3,1},{4,6},{5,7},{6,4},{7,5},{8,10},{9,11},{10,... | collective-permute-start | bytes 319496 | tf_op jit(solution)/shard_map/ppermute | solution.py:151
  92.3 0.7 collective-permute-start.11
  93.0 0.8 collective-permute-start.9
  93.8 1.8 collective-permute-done.10.b
  95.6 2.0 %collective-permute-done.11.c = bf16[64,832]{1,0:T(8,128)(2,1)S(1)} collective-permute-done((bf16[64,832]{1,0:T(8,128)(2,1)S(1)}, bf16[64,832]{1,0:T(8,128)(2,1)S(1)}, u32[]{:S(2)}, u32[]{:S(2)}) %collective-permute-start.11) | collective-permute-done | bytes 106528 | tf_op jit(solution)/shard_map/ppermute | solution.py:151
  97.6 0.3 collective-permute-done.9.a
  97.9 3.5 %shard_map.118 = (f32[64,640]{1,0:T(8,128)}, f32[64,1024]{1,0:T(8,128)}, f32[32,16,128]{2,1,0:T(8,128)S(1)}, f32[32,16,128]{2,1,0:T(8,128)S(1)}) custom-call(s32[1]{0:T(128)} %bitcast.place, f32[64,640]{1,0:T(8,128)S(1)} %get-tuple-element.27.product, f32[64,64]{1,0:T(8,128)S(1)} %get-tuple-element.28.gram, bf16[64,832]{1,0:T(8,128)(2,1)S(1)} %collective-permute-done.9.a, ...), custom_call_target="tpu_custom_call" | custom-call | tf_op jit(solution)/shard_map/pallas_call | solution.py:253
  101.3 2.1 %collective-permute-start.12 = (f32[32,16,128]{2,1,0:T(8,128)S(1)}, f32[32,16,128]{2,1,0:T(8,128)S(1)}, u32[]{:S(2)}, u32[]{:S(2)}) collective-permute-start(f32[32,16,128]{2,1,0:T(8,128)S(1)} %get-tuple-element.32), channel_id=1, source_target_pairs={{0,4},{4,0},{1,5},{5,1},{2,6},{6,2},{3,7},{7,3},{8,12},{12,8},{9,1... | collective-permute-start | bytes 786440 | tf_op jit(solution)/shard_map/ppermute | solution.py:147
  103.4 1.2 collective-permute-done.12
  104.6 14.9 %all_to_all.37.parts = f32[32,16,128]{2,1,0:T(8,128)S(1)} all-to-all(f32[32,16,128]{2,1,0:T(8,128)S(1)} %add.65), channel_id=1, replica_groups=mesh['chip'=32,'core'=2,'snp'=4] {'chip'}, dimensions={0} | all-to-all | bytes 524288 | tf_op jit(solution)/shard_map/all_to_all | solution.py:157
  119.6 0.1 shard_map.119
  119.6 15.0 %all_to_all.38.mine = f32[32,16,128]{2,1,0:T(8,128)S(1)} all-to-all(f32[32,16,128]{2,1,0:T(8,128)S(1)} %shard_map.119), channel_id=1, replica_groups=mesh['chip'=32,'core'=2,'snp'=4] {'chip'}, dimensions={0} | all-to-all | bytes 524288 | tf_op jit(solution)/shard_map/all_to_all | solution.py:159
  134.6 3.3 %collective-permute-start.13 = (f32[32,16,128]{2,1,0:T(8,128)S(1)}, f32[32,16,128]{2,1,0:T(8,128)S(1)}, u32[]{:S(2)}, u32[]{:S(2)}) collective-permute-start(f32[32,16,128]{2,1,0:T(8,128)S(1)} %all_to_all.38.mine), channel_id=1, source_target_pairs={{0,4},{4,0},{1,5},{5,1},{2,6},{6,2},{3,7},{7,3},{8,12},{12,8},{9,1... | collective-permute-start | bytes 786440 | tf_op jit(solution)/shard_map/ppermute | solution.py:147
  137.9 1.2 collective-permute-done.13.other
  139.1 3.1 %shard_map.120 = (f32[64,1024]{1,0:T(8,128)S(1)}, f32[64,640]{1,0:T(8,128)S(1)}, f32[64,64]{1,0:T(8,128)S(1)}, bf16[64,832]{1,0:T(8,128)(2,1)S(1)}) custom-call(s32[1]{0:T(128)} %bitcast.place, f32[32,16,128]{2,1,0:T(8,128)S(1)} %all_to_all.38.mine, f32[32,16,128]{2,1,0:T(8,128)S(1)} %collective-permute-done.13.other, bf16[640,1024]{1,0:T(8,128)(2,1)S(1)} %shard_map.114.x), custom_call_target="tpu_custom_call" | custom-call | tf_op jit(solution)/shard_map/pallas_call | solution.py:253
  142.1 0.5 collective-permute-start.14
  142.6 2.0 %collective-permute-start.15 = (bf16[64,832]{1,0:T(8,128)(2,1)S(1)}, bf16[64,832]{1,0:T(8,128)(2,1)S(1)}, u32[]{:S(2)}, u32[]{:S(2)}) collective-permute-start(bf16[64,832]{1,0:T(8,128)(2,1)S(1)} %get-tuple-element.35), channel_id=1, source_target_pairs={{0,2},{1,3},{2,0},{3,1},{4,6},{5,7},{6,4},{7,5},{8,10},{9,11},{10,... | collective-permute-start | bytes 319496 | tf_op jit(solution)/shard_map/ppermute | solution.py:151
  144.6 1.6 collective-permute-start.16
  146.2 1.8 collective-permute-done.14.a
  148.0 2.0 %collective-permute-done.15.b = bf16[64,832]{1,0:T(8,128)(2,1)S(1)} collective-permute-done((bf16[64,832]{1,0:T(8,128)(2,1)S(1)}, bf16[64,832]{1,0:T(8,128)(2,1)S(1)}, u32[]{:S(2)}, u32[]{:S(2)}) %collective-permute-start.15) | collective-permute-done | bytes 106528 | tf_op jit(solution)/shard_map/ppermute | solution.py:151
  150.0 0.5 collective-permute-done.16.c
  150.5 3.4 %shard_map.121 = (f32[64,640]{1,0:T(8,128)S(1)}, f32[64,1024]{1,0:T(8,128)}, f32[32,16,128]{2,1,0:T(8,128)S(1)}, f32[32,16,128]{2,1,0:T(8,128)S(1)}) custom-call(s32[1]{0:T(128)} %bitcast.place, f32[64,640]{1,0:T(8,128)S(1)} %get-tuple-element.33.product, f32[64,64]{1,0:T(8,128)S(1)} %get-tuple-element.34.gram, ...), custom_call_target="tpu_custom_call" | custom-call | tf_op jit(solution)/shard_map/pallas_call | solution.py:253
  153.9 1.5 collective-permute-start.17
  155.4 1.2 collective-permute-done.17
  156.6 14.9 %all_to_all.39.parts = f32[32,16,128]{2,1,0:T(8,128)S(1)} all-to-all(f32[32,16,128]{2,1,0:T(8,128)S(1)} %add.66), channel_id=1, replica_groups=mesh['chip'=32,'core'=2,'snp'=4] {'chip'}, dimensions={0} | all-to-all | bytes 524288 | tf_op jit(solution)/shard_map/all_to_all | solution.py:157
  171.6 15.0 %all_to_all.40.mine = f32[32,16,128]{2,1,0:T(8,128)S(1)} all-to-all(f32[32,16,128]{2,1,0:T(8,128)S(1)} %shard_map.122), channel_id=1, replica_groups=mesh['chip'=32,'core'=2,'snp'=4] {'chip'}, dimensions={0} | all-to-all | bytes 524288 | tf_op jit(solution)/shard_map/all_to_all | solution.py:159
  186.6 3.3 %collective-permute-start.18 = (f32[32,16,128]{2,1,0:T(8,128)S(1)}, f32[32,16,128]{2,1,0:T(8,128)S(1)}, u32[]{:S(2)}, u32[]{:S(2)}) collective-permute-start(f32[32,16,128]{2,1,0:T(8,128)S(1)} %all_to_all.40.mine), channel_id=1, source_target_pairs={{0,4},{4,0},{1,5},{5,1},{2,6},{6,2},{3,7},{7,3},{8,12},{12,8},{9,1... | collective-permute-start | bytes 786440 | tf_op jit(solution)/shard_map/ppermute | solution.py:147
  189.9 1.2 collective-permute-done.18.other
  191.0 3.2 %shard_map.123 = (f32[64,640]{1,0:T(8,128)}, f32[64,1024]{1,0:T(8,128)}) custom-call(s32[1]{0:T(128)} %bitcast.place, f32[32,16,128]{2,1,0:T(8,128)S(1)} %all_to_all.40.mine, f32[32,16,128]{2,1,0:T(8,128)S(1)} %collective-permute-done.18.other, f32[64,640]{1,0:T(8,128)S(1)} %get-tuple-element.39.samples), custom_call_target="tpu_custom_call" | custom-call | tf_op jit(solution)/shard_map/pallas_call | solution.py:253
  (25 shorter events, 0.2 us)
Async XLA Ops:
  2.1 36.9 %copy-start.4 = (f32[640,20]{0,1:T(8,128)S(1)}, f32[640,20]{0,1:T(8,128)}, u32[]{:S(2)}) copy-start(f32[640,20]{0,1:T(8,128)} %param.11) | copy-start | bytes 153604
  2.1 36.9 %copy-start.5 = (f32[20]{0:T(128)S(1)}, f32[20]{0:T(128)}, u32[]{:S(2)}) copy-start(f32[20]{0:T(128)} %param.12) | copy-start | bytes 244
  2.1 23.2 %all-to-all-start = ((f32[32,16,128]{2,1,0:T(8,128)}), f32[32,16,128]{2,1,0:T(8,128)S(1)}, u32[]{:S(2)}, u32[]{:S(2)}) async-start(f32[32,16,128]{2,1,0:T(8,128)} %broadcast_in_dim.16), calls=%async_computation | async-start | bytes 524288 | tf_op jit(solution)/shard_map/all_to_all | solution.py:182
  14.1 24.9 %copy-start.2 = (bf16[1024,64]{0,1:T(8,128)(2,1)S(1)}, bf16[1024,64]{0,1:T(8,128)(2,1)}, u32[]{:S(2)}) copy-start(bf16[1024,64]{0,1:T(8,128)(2,1)} %param.14) | copy-start | bytes 393220
  25.3 13.7 %collective-permute-start.3 = (f32[32,16,128]{2,1,0:T(8,128)S(1)}, f32[32,16,128]{2,1,0:T(8,128)S(1)}, u32[]{:S(2)}, u32[]{:S(2)}) collective-permute-start(f32[32,16,128]{2,1,0:T(8,128)S(1)} %all-to-all-done.mine), channel_id=1, source_target_pairs={{0,4},{4,0},{1,5},{5,1},{2,6},{6,2},{3,7},{7,3},{8,12},{12,8},{9,1... | collective-permute-start | bytes 786440 | tf_op jit(solution)/shard_map/ppermute | solution.py:147
  29.0 14.0 %copy-start = (f32[4,640]{0,1:T(8,128)S(1)}, f32[4,640]{0,1:T(8,128)}, u32[]{:S(2)}) copy-start(f32[4,640]{0,1:T(8,128)} %copy.15) | copy-start | bytes 30724
  33.9 9.2 %copy-start.1 = (bf16[640,1024]{1,0:T(8,128)(2,1)S(1)}, bf16[640,1024]{1,0:T(8,128)(2,1)}, u32[]{:S(2)}) copy-start(bf16[640,1024]{1,0:T(8,128)(2,1)} %get-tuple-element.24.obs) | copy-start | bytes 3932164
  33.9 7.4 %collective-permute-start = (f32[64,640]{1,0:T(8,128)}, f32[64,640]{1,0:T(8,128)S(1)}, u32[]{:S(2)}, u32[]{:S(2)}) collective-permute-start(f32[64,640]{1,0:T(8,128)} %get-tuple-element.23.own), channel_id=1, source_target_pairs={{0,1},{1,2},{2,3},{3,0},{4,5},{5,6},{6,7},{7,4},{8,9},{9,10},{10,1... | collective-permute-start | bytes 491528 | tf_op jit(solution)/shard_map/ppermute | solution.py:151
  35.2 10.8 %collective-permute-start.1 = (f32[64,640]{1,0:T(8,128)}, f32[64,640]{1,0:T(8,128)S(1)}, u32[]{:S(2)}, u32[]{:S(2)}) collective-permute-start(f32[64,640]{1,0:T(8,128)} %get-tuple-element.23.own), channel_id=1, source_target_pairs={{0,2},{1,3},{2,0},{3,1},{4,6},{5,7},{6,4},{7,5},{8,10},{9,11},{10,... | collective-permute-start | bytes 491528 | tf_op jit(solution)/shard_map/ppermute | solution.py:151
  37.8 8.1 %collective-permute-start.2 = (f32[64,640]{1,0:T(8,128)}, f32[64,640]{1,0:T(8,128)S(1)}, u32[]{:S(2)}, u32[]{:S(2)}) collective-permute-start(f32[64,640]{1,0:T(8,128)} %get-tuple-element.23.own), channel_id=1, source_target_pairs={{0,3},{1,0},{2,1},{3,2},{4,7},{5,4},{6,5},{7,6},{8,11},{9,8},{10,9... | collective-permute-start | bytes 491528 | tf_op jit(solution)/shard_map/ppermute | solution.py:151
  39.5 7.7 %collective-permute-start.4 = (f32[64,128]{1,0:T(8,128)S(1)}, f32[64,128]{1,0:T(8,128)S(1)}, u32[]{:S(2)}, u32[]{:S(2)}) collective-permute-start(f32[64,128]{1,0:T(8,128)S(1)} %shard_map.113.q0), channel_id=1, source_target_pairs={{0,1},{1,2},{2,3},{3,0},{4,5},{5,6},{6,7},{7,4},{8,9},{9,10},{10,1... | collective-permute-start | bytes 98312 | tf_op jit(solution)/shard_map/ppermute | solution.py:151
  39.9 7.2 %collective-permute-start.5 = (f32[64,128]{1,0:T(8,128)S(1)}, f32[64,128]{1,0:T(8,128)S(1)}, u32[]{:S(2)}, u32[]{:S(2)}) collective-permute-start(f32[64,128]{1,0:T(8,128)S(1)} %shard_map.113.q0), channel_id=1, source_target_pairs={{0,2},{1,3},{2,0},{3,1},{4,6},{5,7},{6,4},{7,5},{8,10},{9,11},{10,... | collective-permute-start | bytes 98312 | tf_op jit(solution)/shard_map/ppermute | solution.py:151
  41.3 5.8 %collective-permute-start.6 = (f32[64,128]{1,0:T(8,128)S(1)}, f32[64,128]{1,0:T(8,128)S(1)}, u32[]{:S(2)}, u32[]{:S(2)}) collective-permute-start(f32[64,128]{1,0:T(8,128)S(1)} %shard_map.113.q0), channel_id=1, source_target_pairs={{0,3},{1,0},{2,1},{3,2},{4,7},{5,4},{6,5},{7,6},{8,11},{9,8},{10,9... | collective-permute-start | bytes 98312 | tf_op jit(solution)/shard_map/ppermute | solution.py:151
  43.0 4.2 %copy-start.3 = (f32[64,640]{1,0:T(8,128)S(1)}, f32[64,640]{1,0:T(8,128)}, u32[]{:S(2)}) copy-start(f32[64,640]{1,0:T(8,128)} %get-tuple-element.23.own) | copy-start | bytes 491524
  48.9 2.2 %collective-permute-start.7 = (f32[32,16,128]{2,1,0:T(8,128)S(1)}, f32[32,16,128]{2,1,0:T(8,128)S(1)}, u32[]{:S(2)}, u32[]{:S(2)}) collective-permute-start(f32[32,16,128]{2,1,0:T(8,128)S(1)} %get-tuple-element.26), channel_id=1, source_target_pairs={{0,4},{4,0},{1,5},{5,1},{2,6},{6,2},{3,7},{7,3},{8,12},{12,8},{9,1... | collective-permute-start | bytes 786440 | tf_op jit(solution)/shard_map/ppermute | solution.py:147
  81.4 4.5 %collective-permute-start.8 = (f32[32,16,128]{2,1,0:T(8,128)S(1)}, f32[32,16,128]{2,1,0:T(8,128)S(1)}, u32[]{:S(2)}, u32[]{:S(2)}) collective-permute-start(f32[32,16,128]{2,1,0:T(8,128)S(1)} %all_to_all.36.mine), channel_id=1, source_target_pairs={{0,4},{4,0},{1,5},{5,1},{2,6},{6,2},{3,7},{7,3},{8,12},{12,8},{9,1... | collective-permute-start | bytes 786440 | tf_op jit(solution)/shard_map/ppermute | solution.py:147
  88.9 6.7 %collective-permute-start.10 = (bf16[64,832]{1,0:T(8,128)(2,1)S(1)}, bf16[64,832]{1,0:T(8,128)(2,1)S(1)}, u32[]{:S(2)}, u32[]{:S(2)}) collective-permute-start(bf16[64,832]{1,0:T(8,128)(2,1)S(1)} %get-tuple-element.29), channel_id=1, source_target_pairs={{0,2},{1,3},{2,0},{3,1},{4,6},{5,7},{6,4},{7,5},{8,10},{9,11},{10,... | collective-permute-start | bytes 319496 | tf_op jit(solution)/shard_map/ppermute | solution.py:151
  92.3 5.2 %collective-permute-start.11 = (bf16[64,832]{1,0:T(8,128)(2,1)S(1)}, bf16[64,832]{1,0:T(8,128)(2,1)S(1)}, u32[]{:S(2)}, u32[]{:S(2)}) collective-permute-start(bf16[64,832]{1,0:T(8,128)(2,1)S(1)} %get-tuple-element.29), channel_id=1, source_target_pairs={{0,3},{1,0},{2,1},{3,2},{4,7},{5,4},{6,5},{7,6},{8,11},{9,8},{10,9... | collective-permute-start | bytes 319496 | tf_op jit(solution)/shard_map/ppermute | solution.py:151
  93.0 4.9 %collective-permute-start.9 = (bf16[64,832]{1,0:T(8,128)(2,1)S(1)}, bf16[64,832]{1,0:T(8,128)(2,1)S(1)}, u32[]{:S(2)}, u32[]{:S(2)}) collective-permute-start(bf16[64,832]{1,0:T(8,128)(2,1)S(1)} %get-tuple-element.29), channel_id=1, source_target_pairs={{0,1},{1,2},{2,3},{3,0},{4,5},{5,6},{6,7},{7,4},{8,9},{9,10},{10,1... | collective-permute-start | bytes 319496 | tf_op jit(solution)/shard_map/ppermute | solution.py:151
  101.3 3.2 %collective-permute-start.12 = (f32[32,16,128]{2,1,0:T(8,128)S(1)}, f32[32,16,128]{2,1,0:T(8,128)S(1)}, u32[]{:S(2)}, u32[]{:S(2)}) collective-permute-start(f32[32,16,128]{2,1,0:T(8,128)S(1)} %get-tuple-element.32), channel_id=1, source_target_pairs={{0,4},{4,0},{1,5},{5,1},{2,6},{6,2},{3,7},{7,3},{8,12},{12,8},{9,1... | collective-permute-start | bytes 786440 | tf_op jit(solution)/shard_map/ppermute | solution.py:147
  134.6 4.5 %collective-permute-start.13 = (f32[32,16,128]{2,1,0:T(8,128)S(1)}, f32[32,16,128]{2,1,0:T(8,128)S(1)}, u32[]{:S(2)}, u32[]{:S(2)}) collective-permute-start(f32[32,16,128]{2,1,0:T(8,128)S(1)} %all_to_all.38.mine), channel_id=1, source_target_pairs={{0,4},{4,0},{1,5},{5,1},{2,6},{6,2},{3,7},{7,3},{8,12},{12,8},{9,1... | collective-permute-start | bytes 786440 | tf_op jit(solution)/shard_map/ppermute | solution.py:147
  142.1 5.9 %collective-permute-start.14 = (bf16[64,832]{1,0:T(8,128)(2,1)S(1)}, bf16[64,832]{1,0:T(8,128)(2,1)S(1)}, u32[]{:S(2)}, u32[]{:S(2)}) collective-permute-start(bf16[64,832]{1,0:T(8,128)(2,1)S(1)} %get-tuple-element.35), channel_id=1, source_target_pairs={{0,1},{1,2},{2,3},{3,0},{4,5},{5,6},{6,7},{7,4},{8,9},{9,10},{10,1... | collective-permute-start | bytes 319496 | tf_op jit(solution)/shard_map/ppermute | solution.py:151
  142.6 7.4 %collective-permute-start.15 = (bf16[64,832]{1,0:T(8,128)(2,1)S(1)}, bf16[64,832]{1,0:T(8,128)(2,1)S(1)}, u32[]{:S(2)}, u32[]{:S(2)}) collective-permute-start(bf16[64,832]{1,0:T(8,128)(2,1)S(1)} %get-tuple-element.35), channel_id=1, source_target_pairs={{0,2},{1,3},{2,0},{3,1},{4,6},{5,7},{6,4},{7,5},{8,10},{9,11},{10,... | collective-permute-start | bytes 319496 | tf_op jit(solution)/shard_map/ppermute | solution.py:151
  144.6 5.9 %collective-permute-start.16 = (bf16[64,832]{1,0:T(8,128)(2,1)S(1)}, bf16[64,832]{1,0:T(8,128)(2,1)S(1)}, u32[]{:S(2)}, u32[]{:S(2)}) collective-permute-start(bf16[64,832]{1,0:T(8,128)(2,1)S(1)} %get-tuple-element.35), channel_id=1, source_target_pairs={{0,3},{1,0},{2,1},{3,2},{4,7},{5,4},{6,5},{7,6},{8,11},{9,8},{10,9... | collective-permute-start | bytes 319496 | tf_op jit(solution)/shard_map/ppermute | solution.py:151
  153.9 2.7 %collective-permute-start.17 = (f32[32,16,128]{2,1,0:T(8,128)S(1)}, f32[32,16,128]{2,1,0:T(8,128)S(1)}, u32[]{:S(2)}, u32[]{:S(2)}) collective-permute-start(f32[32,16,128]{2,1,0:T(8,128)S(1)} %get-tuple-element.38), channel_id=1, source_target_pairs={{0,4},{4,0},{1,5},{5,1},{2,6},{6,2},{3,7},{7,3},{8,12},{12,8},{9,1... | collective-permute-start | bytes 786440 | tf_op jit(solution)/shard_map/ppermute | solution.py:147
  186.6 4.5 %collective-permute-start.18 = (f32[32,16,128]{2,1,0:T(8,128)S(1)}, f32[32,16,128]{2,1,0:T(8,128)S(1)}, u32[]{:S(2)}, u32[]{:S(2)}) collective-permute-start(f32[32,16,128]{2,1,0:T(8,128)S(1)} %all_to_all.40.mine), channel_id=1, source_target_pairs={{0,4},{4,0},{1,5},{5,1},{2,6},{6,2},{3,7},{7,3},{8,12},{12,8},{9,1... | collective-permute-start | bytes 786440 | tf_op jit(solution)/shard_map/ppermute | solution.py:147

commit v4 on v2

--- a/solution.py
+++ b/solution.py
@@ -13,6 +13,7 @@
 BLOCKS = 16
 LANES = 128
 SUB = 8
+GROUP = 32
 F32 = jnp.float32
 BF16 = jnp.bfloat16
 HIGH = lax.Precision.HIGHEST
@@ -174,91 +175,228 @@
         width = sketch.shape[1]
         sample_count = row_count * samp
         snp_count = col_width * snp
-        core = lax.axis_index("core")
-        place = core.reshape(1).astype(jnp.int32)
-        samp_index = lax.axis_index("chip") * 2 + core
-
-        right_mine = lax.all_to_all(
-            jnp.broadcast_to(right_factors[None], (chips, *right_factors.shape)), "chip", 0, 0
-        )
-        right_other = swap(right_mine)
-
-        batch_range = jnp.arange(BATCHES, dtype=jnp.int32)
+        place = lax.axis_index(("chip", "core", "snp")).reshape(1).astype(jnp.int32)
         local_blocks = col_width // BLOCK
-        block_range = lax.axis_index("snp") * local_blocks + jnp.arange(
-            local_blocks, dtype=jnp.int32
-        )
-        ends = jnp.sum(
-            jnp.where(batch_range[:, None] <= batch_range[None, :], batch_sizes[:, None], 0), axis=0
-        )
-        row_ids = samp_index * row_count + jnp.arange(row_count, dtype=jnp.int32)
-        batch_of = jnp.sum((row_ids[:, None] >= ends[None, :]).astype(jnp.int32), axis=1)
-        missing = jnp.sum(
-            (
-                (batch_of[:, None, None] == missing_batch[None, None, :])
-                & (block_range[None, :, None] == missing_block[None, None, :])
-            ).astype(F32),
-            axis=2,
-        )
-        observed = (genotype.astype(F32) - 2.0 * freqs[None, :]).astype(BF16)
-        weighted = left_factors * singular[None, :]
-
-        def build_kernel(place, obs, miss, weight, mine, other, omega, x_out, start):
-            first = place[0] == 0
-            r_mine, r_other = mine[...], other[...]
-            low = jnp.where(first, r_mine, r_other)
-            high = jnp.where(first, r_other, r_mine)
-            right = jnp.stack([low, high], axis=1).reshape(col_width, rank)
-            lowrank = exact_dot(weight[...], right, 1, 1)
-            pieces = []
-            for j in range(local_blocks):
-                at = slice(BLOCK * j, BLOCK * (j + 1))
-                gone = jnp.broadcast_to(miss[:, j : j + 1], (row_count, BLOCK)) > 0.5
-                pieces.append(jnp.where(gone, lowrank[:, at], obs[:, at].astype(F32)))
-            x = jnp.concatenate(pieces, axis=1).astype(BF16)
-            x_out[...] = x
-            start[...] = lax.dot_general(
-                omega[...], x, (((1,), (1,)), ((), ())), preferred_element_type=F32
-            )
-
-        def call_with_place(body, outs, *operands):
-            specs = [pl.BlockSpec(memory_space=pltpu.SMEM)] + [
+        omega = sketch.T
+
+        def core_of(place):
+            return place[0] // snp % 2
+
+        def call_with_place(body, outs, *operands, scalars=(), out_specs=None, cost=None):
+            smem = pl.BlockSpec(memory_space=pltpu.SMEM)
+            specs = [smem] * (1 + len(scalars)) + [
                 pl.BlockSpec(memory_space=pltpu.VMEM) for _ in operands
             ]
+            more = {} if out_specs is None else {"out_specs": out_specs}
             return pl.pallas_call(
                 body,
                 out_shape=outs,
                 in_specs=specs,
+                cost_estimate=cost,
                 compiler_params=pltpu.CompilerParams(vmem_limit_bytes=48 * 1024 * 1024),
-            )(place, *operands)
-
-        matrix, start = call_with_place(
+                **more,
+            )(place, *scalars, *operands)
+
+        def batch_ids(place, sizes, shape, axis):
+            ids = lax.broadcasted_iota(jnp.int32, shape, axis) + place[0] // snp * row_count
+            batch = jnp.zeros(shape, jnp.int32)
+            end = jnp.int32(0)
+            for b in range(BATCHES - 1):
+                end = end + sizes[b]
+                batch = batch + (ids >= end).astype(jnp.int32)
+            return batch
+
+        def gone_in(bits, batch):
+            return ((jnp.broadcast_to(bits, batch.shape) >> batch) & 1) == 1
+
+        chunk = LANES
+
+        def observe_kernel(
+            place, sizes_in, batch_in, block_in, geno_in, freq_in, om_in,
+            obs, start, bits,
+            sizes, tile_batch, tile_block, geno, freq, om, sems,
+        ):
+            copies = [
+                pltpu.make_async_copy(source, target, sems.at[i])
+                for i, (source, target) in enumerate(
+                    [
+                        (batch_in, tile_batch),
+                        (block_in, tile_block),
+                        (sizes_in, sizes),
+                        (freq_in, freq),
+                    ]
+                    + [
+                        (geno_in.at[pl.ds(low, chunk)], geno.at[pl.ds(low, chunk)])
+                        for low in range(0, row_count, chunk)
+                    ]
+                    + [(om_in, om)]
+                )
+            ]
+            for copy in copies:
+                copy.start()
+            for block in range(BLOCKS):
+                bits[block] = 0
+            copies[0].wait()
+            copies[1].wait()
+            for i in range(tile_batch.shape[0]):
+                block = tile_block[i]
+                bits[block] = bits[block] | (1 << tile_batch[i])
+            copies[2].wait()
+            copies[3].wait()
+            batch = batch_ids(place, sizes, (row_count, LANES), 0)
+            own_bits = [bits[place[0] % snp * local_blocks + j] for j in range(local_blocks)]
+            for n, top in enumerate(range(0, row_count, chunk)):
+                copies[4 + n].wait()
+                rows = slice(top, top + chunk)
+                for j in range(local_blocks):
+                    gone = gone_in(own_bits[j], batch[rows])
+                    for low in range(BLOCK * j, BLOCK * (j + 1), LANES):
+                        at = slice(low, low + LANES)
+                        values = geno[rows, at].astype(F32) - 2.0 * freq[:, at]
+                        obs[rows, at] = jnp.where(gone, 0.0, values).astype(BF16)
+            copies[-1].wait()
+            start[...] = lax.dot_general(
+                om[...], obs[...], (((1,), (1,)), ((), ())), preferred_element_type=F32
+            )
+
+        vmem = pl.BlockSpec(memory_space=pltpu.VMEM)
+        smem = pl.BlockSpec(memory_space=pltpu.SMEM)
+        tiles = missing_batch.shape
+        observed, start, bits = pl.pallas_call(
+            observe_kernel,
+            out_shape=(
+                shape_of((row_count, col_width), BF16),
+                shape_of((width, row_count)),
+                shape_of((BLOCKS,), jnp.int32),
+            ),
+            in_specs=[smem] + [pl.BlockSpec(memory_space=pltpu.HBM)] * 6,
+            out_specs=(vmem, vmem, smem),
+            scratch_shapes=[
+                pltpu.SMEM(batch_sizes.shape, jnp.int32),
+                pltpu.SMEM(tiles, jnp.int32),
+                pltpu.SMEM(tiles, jnp.int32),
+                pltpu.VMEM((row_count, col_width), jnp.int32),
+                pltpu.VMEM((1, col_width), F32),
+                pltpu.VMEM((width, col_width), BF16),
+                pltpu.SemaphoreType.DMA((5 + row_count // chunk,)),
+            ],
+            compiler_params=pltpu.CompilerParams(vmem_limit_bytes=63 * 1024 * 1024),
+        )(
+            place,
+            batch_sizes,
+            missing_batch,
+            missing_block,
+            genotype,
+            freqs.reshape(1, col_width),
+            omega,
+        )
+
+        def pack_kernel(place, bits, mine, other, spread):
+            del bits
+            first = core_of(place) == 0
+            low = jnp.where(first, mine[...], other[...])
+            high = jnp.where(first, other[...], mine[...])
+            fill = jnp.zeros((SUB, GROUP - rank), F32)
+            pieces = []
+            for part in (low, high):
+                for top in range(0, part.shape[0], SUB):
+                    pieces += [part[top : top + SUB], fill]
+            tile = jnp.concatenate(pieces, axis=1)
+            spread[...] = jnp.broadcast_to(tile[None], spread.shape)
+
+        right_tiles = lax.all_to_all(
+            call_with_place(
+                pack_kernel,
+                shape_of((chips, SUB, LANES)),
+                right_factors,
+                swap(right_factors),
+                scalars=(bits,),
+            ),
+            "chip",
+            0,
+            0,
+        )
+        start_others = snp_others(start)
+
+        def right_rows(tiles):
+            value = tiles[...]
+            parts = [value[:, :, g : g + GROUP] for g in range(0, LANES, GROUP)]
+            return jnp.stack(parts, axis=1).reshape(col_width, GROUP)
+
+        def weight_rows(scale, left):
+            rows = [left[r : r + 1, :] * scale[r] for r in range(rank)]
+            return jnp.concatenate(
+                [*rows, jnp.zeros((GROUP - rank, row_count), F32)], axis=0
+            )
+
+        def mix_kernel(place, tiles, om, mixed):
+            right = right_rows(tiles)
+            pieces = [
+                exact_dot(
+                    om[:, BLOCK * j : BLOCK * (j + 1)].astype(F32),
+                    right[BLOCK * j : BLOCK * (j + 1)],
+                    1,
+                    0,
+                )
+                for j in range(local_blocks)
+            ]
+            mixed[...] = jnp.concatenate(pieces, axis=1)
+
+        def build_kernel(place, sizes, bits, scale, obs, left, tiles, x_out):
+            right = right_rows(tiles)
+            weight = weight_rows(scale, left).T
+            batch = batch_ids(place, sizes, (row_count, BLOCK), 0)
+            for j in range(local_blocks):
+                at = slice(BLOCK * j, BLOCK * (j + 1))
+                lowrank = exact_dot(weight, right[at], 1, 1)
+                gone = gone_in(bits[place[0] % snp * local_blocks + j], batch)
+                x_out[:, at] = jnp.where(gone, lowrank, obs[:, at].astype(F32)).astype(BF16)
+
+        mixed = call_with_place(
+            mix_kernel,
+            shape_of((width, local_blocks * GROUP)),
+            right_tiles,
+            omega,
+        )
+        mixed_others = snp_others(mixed)
+        left_rows = left_factors.T
+        matrix = call_with_place(
             build_kernel,
-            (shape_of((row_count, col_width), BF16), shape_of((width, row_count))),
+            shape_of((row_count, col_width), BF16),
             observed,
-            missing,
-            weighted,
-            right_mine,
-            right_other,
-            sketch.T,
+            left_rows,
+            right_tiles,
+            scalars=(batch_sizes, bits, singular),
         )
 
         part_shape = shape_of((chips, 2 * SUB, LANES))
         packed = row_count + 3 * width
 
-        def first_kernel(place, own, a, b, c, x, samples_out, mine, other):
+        def first_kernel(
+            place, sizes, bits, scale, own, a, b, c, q0, q1, q2, q3, left, x,
+            samples_out, mine, other,
+        ):
             samples = own[...] + a[...] + b[...] + c[...]
+            batch = batch_ids(place, sizes, (1, row_count), 1)
+            weight = weight_rows(scale, left)
+            for k, q in enumerate((q0, q1, q2, q3)):
+                source = (place[0] + (snp - k)) % snp
+                masked = [
+                    jnp.where(gone_in(bits[source * local_blocks + j], batch), weight, 0.0)
+                    for j in range(local_blocks)
+                ]
+                samples = samples + exact_dot(q[...], jnp.concatenate(masked, axis=0), 1, 0)
             samples_out[...] = samples
             write_send(
                 split_dot(samples, x[...], 0),
                 exact_dot(samples, samples, 1, 1),
-                place[0],
+                core_of(place),
                 mine,
                 other,
             )
 
         def forward_kernel(place, mine, other, x, raw_out, product_out, gram_out, wire):
-            columns, gram = read_sum(mine, other, place[0], col_width)
+            columns, gram = read_sum(mine, other, core_of(place), col_width)
             raw = exact_dot(inverse_factor(gram / sample_count, True), columns, 1, 0)
             raw_out[...] = raw
             product = split_dot(raw, x[...], 1)
@@ -285,13 +423,13 @@
             write_send(
                 split_dot(samples, x[...], 0),
                 exact_dot(samples, samples, 1, 1),
-                place[0],
+                core_of(place),
                 mine,
                 other,
             )
 
         def last_kernel(place, mine, other, samples, basis, projection):
-            columns, gram = read_sum(mine, other, place[0], col_width)
+            columns, gram = read_sum(mine, other, core_of(place), col_width)
             factor = inverse_factor(gram / sample_count, True)
             basis[...] = exact_dot(factor, samples[...], 1, 0)
             projection[...] = exact_dot(factor / math.sqrt(sample_count), columns, 1, 0)
@@ -302,8 +440,12 @@
             first_kernel,
             (samples_shape, part_shape, part_shape),
             start,
-            *snp_others(start),
+            *start_others,
+            mixed,
+            *mixed_others,
+            left_rows,
             matrix,
+            scalars=(batch_sizes, bits, singular),
         )
         columns = None
         for _ in range(ITERS):

time: 192 us -> 190 us (0.990)
  waiting for transfers between devices: 36.5 us -> 25.9 us
  starting transfers between devices: 32.4 us -> 41.9 us
  Pallas kernels: 19.7 us -> 26.5 us
  other arithmetic: 6.15 us -> 0.1 us
    ppermute x9 -> x12, waiting for transfers between devices: 26.1 us -> 12.8 us  [snp_others(): lax.ppermute(value, 'snp', [(i, (i + k) % snp) for i in range(snp)])]
    ppermute x9 -> x12, starting transfers between devices: 6.89 us -> 15.2 us  [snp_others(): lax.ppermute(value, 'snp', [(i, (i + k) % snp) for i in range(snp)])]
    pallas_call x7 -> x10, Pallas kernels: 19.5 us -> 26.4 us  [the longest x9 23.2 us: call_with_place(): pl.pallas_call(body, out_shape=outs, in_specs=specs, cost_estimate=cost,...]
    ppermute x7, starting transfers between devices: 13.5 us -> 17.3 us  [swap(): return lax.ppermute(value, 'core', [(0, 1), (1, 0)])]
    all_to_all x1, waiting for transfers between devices: 2.52 us -> 6.07 us  [on_device(): lax.all_to_all(call_with_place(pack_kernel, shape_of((chips, SUB, LANES))...]
    all_to_all x1, starting transfers between devices: 12 us -> 9.3 us  [on_device(): lax.all_to_all(call_with_place(pack_kernel, shape_of((chips, SUB, LANES))...]
    convert_element_type x1 -> x0, other arithmetic: 2.09 us -> none  [on_device(): observed = (genotype.astype(F32) - 2.0 * freqs[None, :]).astype(BF16)]
  transfers between devices with their start and end apart: 17 -> 20, of which waited for: 17 -> 12; matrix products, arithmetic and copies ran while one was open for 3% -> 0% of each run, Pallas kernels for 0% -> 4%
where the time goes in v4:
time: 190 us; the launch traced here: 189 us
  blocking collectives  91.5 us (48%)
  starting transfers between devices  41.9 us (22%)
  Pallas kernels  26.5 us (14%)
  waiting for transfers between devices  25.9 us (14%)
  local copies, waits for them, and re-layouts  2.64 us (1%)
    all_to_all x3, blocking collectives, samp_sum(): got = lax.all_to_all(send, 'chip', 0, 0)  46.5 us
    all_to_all x3, blocking collectives, samp_sum(): whole = lax.all_to_all(spread, 'chip', 0, 0)  45 us
    pallas_call x9, Pallas kernels, call_with_place(): pl.pallas_call(body, out_shape=outs, in_specs=specs, cost_estimate=cost,...  23.2 us
    ppermute x7, starting transfers between devices, swap(): return lax.ppermute(value, 'core', [(0, 1), (1, 0)])  17.3 us
    ppermute x12, starting transfers between devices, snp_others(): lax.ppermute(value, 'snp', [(i, (i + k) % snp) for i in range(snp)])  15.2 us
    ppermute x12, waiting for transfers between devices, snp_others(): lax.ppermute(value, 'snp', [(i, (i + k) % snp) for i in range(snp)])  12.8 us
    all_to_all x1, starting transfers between devices, on_device(): lax.all_to_all(call_with_place(pack_kernel, shape_of((chips, SUB, LANES))...  9.3 us
    ppermute x7, waiting for transfers between devices, swap(): return lax.ppermute(value, 'core', [(0, 1), (1, 0)])  6.98 us
  transfers between devices with their start and end apart: 20, of which 12 were waited for; matrix products, arithmetic and copies ran while one was open for 0% of the time, Pallas kernels for 4%

profile of v4, /device:TPU:1, one launch (start us, length us, event | category | flops | bytes accessed | tf_op | source)
XLA Modules:
  0.0 189.3 jit_solution(1759670939858504000)
XLA Ops:
  0.6 3.3 %collective-permute-start.3 = (f32[16,20]{1,0:T(8,128)}, f32[16,20]{1,0:T(8,128)S(1)}, u32[]{:S(2)}, u32[]{:S(2)}) collective-permute-start(f32[16,20]{1,0:T(8,128)} %mine.1), channel_id=1, source_target_pairs={{0,4},{4,0},{1,5},{5,1},{2,6},{6,2},{3,7},{7,3},{8,12},{12,8},{9,1... | collective-permute-start | bytes 3848 | tf_op jit(solution)/shard_map/ppermute | solution.py:147
  4.0 3.2 %shard_map.112 = (bf16[640,1024]{1,0:T(8,128)(2,1)}, f32[64,640]{1,0:T(8,128)}, s32[16]{0:T(128)}) custom-call(s32[1]{0:T(128)} %bitcast.place, s32[12]{0:T(128)} %sizes.3, s32[48]{0:T(128)} %batch_in.1, s32[48]{0:T(128)} %block_in.1, s32[640,1024]{1,0:T(8,128)} %geno_in.1, f32[1,1024]{1,0:T(1,128)} %bitcast.11, bf16[64,1024]{1,0:T(8,128)(2,1)} %bitcast.7), custom_call_target="tpu_custom_call" | custom-call | tf_op jit(solution)/shard_map/pallas_call | solution.py:265
  7.2 0.0 collective-permute-done.3.other
  7.2 0.0 copy-start.6
  7.2 0.6 copy-done.6
  7.9 1.3 shard_map.113
  9.2 9.3 %all-to-all-start = ((f32[32,8,128]{2,1,0:T(8,128)}), f32[32,8,128]{2,1,0:T(8,128)S(1)}, u32[]{:S(2)}, u32[]{:S(2)}) async-start(f32[32,8,128]{2,1,0:T(8,128)} %shard_map.113), calls=%async_computation | async-start | bytes 262144 | tf_op jit(solution)/shard_map/all_to_all | solution.py:307
  18.5 2.8 %collective-permute-start.2 = (f32[64,640]{1,0:T(8,128)}, f32[64,640]{1,0:T(8,128)S(1)}, u32[]{:S(2)}, u32[]{:S(2)}) collective-permute-start(f32[64,640]{1,0:T(8,128)} %get-tuple-element.25.own), channel_id=1, source_target_pairs={{0,3},{1,0},{2,1},{3,2},{4,7},{5,4},{6,5},{7,6},{8,11},{9,8},{10,9... | collective-permute-start | bytes 491528 | tf_op jit(solution)/shard_map/ppermute | solution.py:151
  21.3 0.4 collective-permute-start.1
  21.6 0.7 collective-permute-start
  22.3 6.1 %all-to-all-done.tiles = f32[32,8,128]{2,1,0:T(8,128)S(1)} async-done(((f32[32,8,128]{2,1,0:T(8,128)}), f32[32,8,128]{2,1,0:T(8,128)S(1)}, u32[]{:S(2)}, u32[]{:S(2)}) %all-to-all-start) | async-done | bytes 131104 | tf_op jit(solution)/shard_map/all_to_all | solution.py:307
  28.4 0.5 shard_map.114.q0
  28.9 2.8 %collective-permute-start.6 = (f32[64,128]{1,0:T(8,128)S(1)}, f32[64,128]{1,0:T(8,128)S(1)}, u32[]{:S(2)}, u32[]{:S(2)}) collective-permute-start(f32[64,128]{1,0:T(8,128)S(1)} %shard_map.114.q0), channel_id=1, source_target_pairs={{0,3},{1,0},{2,1},{3,2},{4,7},{5,4},{6,5},{7,6},{8,11},{9,8},{10,9... | collective-permute-start | bytes 98312 | tf_op jit(solution)/shard_map/ppermute | solution.py:151
  31.7 0.3 collective-permute-start.5
  32.1 0.0 collective-permute-done.2.c
  32.1 0.7 collective-permute-start.4
  32.8 1.3 copy-done
  34.1 0.7 copy-done.7
  34.8 2.9 %shard_map.115.x = bf16[640,1024]{1,0:T(8,128)(2,1)S(1)} custom-call(s32[1]{0:T(128)} %bitcast.place, s32[12]{0:T(128)S(1)} %copy-done.5, s32[16]{0:T(128)S(1)} %copy-done.7, f32[20]{0:T(128)S(1)} %copy-done.8, bf16[640,1024]{1,0:T(8,128)(2,1)S(1)} %copy-done, f32[20,640]{1,0:T(8,128)S(1)} %bitcast.9, f32[32,8,128]{2,1,0:T(8,128)S(1)} %all-to-all-done.tiles), custom_call_target="tpu_custom_call" | custom-call | tf_op jit(solution)/shard_map/pallas_call | solution.py:191
  37.7 0.0 collective-permute-done.1.b
  37.7 0.0 collective-permute-done.a
  37.7 0.0 collective-permute-done.6.q3
  37.7 0.0 collective-permute-done.5.q2
  37.7 0.0 collective-permute-done.4.q1
  37.7 0.0 copy-done.3
  37.7 2.2 %shard_map.116 = (f32[64,640]{1,0:T(8,128)}, f32[32,16,128]{2,1,0:T(8,128)S(1)}, f32[32,16,128]{2,1,0:T(8,128)S(1)}) custom-call(s32[1]{0:T(128)} %bitcast.place, s32[12]{0:T(128)S(1)} %copy-done.5, s32[16]{0:T(128)S(1)} %copy-done.7, f32[20]{0:T(128)S(1)} %copy-done.8, f32[64,640]{1,0:T(8,128)S(1)} %copy-done.3, f32[64,640]{1,0:T(8,128)S(1)} %collective-permute-done.a, ...), custom_call_target="tpu_custom_call" | custom-call | tf_op jit(solution)/shard_map/pallas_call | solution.py:191
  40.0 2.3 %collective-permute-start.7 = (f32[32,16,128]{2,1,0:T(8,128)S(1)}, f32[32,16,128]{2,1,0:T(8,128)S(1)}, u32[]{:S(2)}, u32[]{:S(2)}) collective-permute-start(f32[32,16,128]{2,1,0:T(8,128)S(1)} %get-tuple-element.28), channel_id=1, source_target_pairs={{0,4},{4,0},{1,5},{5,1},{2,6},{6,2},{3,7},{7,3},{8,12},{12,8},{9,1... | collective-permute-start | bytes 786440 | tf_op jit(solution)/shard_map/ppermute | solution.py:147
  42.2 1.2 collective-permute-done.7
  43.4 16.6 %all_to_all.35.parts = f32[32,16,128]{2,1,0:T(8,128)S(1)} all-to-all(f32[32,16,128]{2,1,0:T(8,128)S(1)} %add.17), channel_id=1, replica_groups=mesh['chip'=32,'core'=2,'snp'=4] {'chip'}, dimensions={0} | all-to-all | bytes 524288 | tf_op jit(solution)/shard_map/all_to_all | solution.py:157
  60.1 0.1 shard_map.117
  60.1 15.0 %all_to_all.36.mine = f32[32,16,128]{2,1,0:T(8,128)S(1)} all-to-all(f32[32,16,128]{2,1,0:T(8,128)S(1)} %shard_map.117), channel_id=1, replica_groups=mesh['chip'=32,'core'=2,'snp'=4] {'chip'}, dimensions={0} | all-to-all | bytes 524288 | tf_op jit(solution)/shard_map/all_to_all | solution.py:159
  75.1 3.3 %collective-permute-start.8 = (f32[32,16,128]{2,1,0:T(8,128)S(1)}, f32[32,16,128]{2,1,0:T(8,128)S(1)}, u32[]{:S(2)}, u32[]{:S(2)}) collective-permute-start(f32[32,16,128]{2,1,0:T(8,128)S(1)} %all_to_all.36.mine), channel_id=1, source_target_pairs={{0,4},{4,0},{1,5},{5,1},{2,6},{6,2},{3,7},{7,3},{8,12},{12,8},{9,1... | collective-permute-start | bytes 786440 | tf_op jit(solution)/shard_map/ppermute | solution.py:147
  78.4 1.2 collective-permute-done.8.other
  79.6 3.1 %shard_map.118 = (f32[64,1024]{1,0:T(8,128)S(1)}, f32[64,640]{1,0:T(8,128)S(1)}, f32[64,64]{1,0:T(8,128)S(1)}, bf16[64,832]{1,0:T(8,128)(2,1)S(1)}) custom-call(s32[1]{0:T(128)} %bitcast.place, f32[32,16,128]{2,1,0:T(8,128)S(1)} %all_to_all.36.mine, f32[32,16,128]{2,1,0:T(8,128)S(1)} %collective-permute-done.8.other, bf16[640,1024]{1,0:T(8,128)(2,1)S(1)} %shard_map.115.x), custom_call_target="tpu_custom_call" | custom-call | tf_op jit(solution)/shard_map/pallas_call | solution.py:191
  82.6 2.9 %collective-permute-start.11 = (bf16[64,832]{1,0:T(8,128)(2,1)S(1)}, bf16[64,832]{1,0:T(8,128)(2,1)S(1)}, u32[]{:S(2)}, u32[]{:S(2)}) collective-permute-start(bf16[64,832]{1,0:T(8,128)(2,1)S(1)} %get-tuple-element.31), channel_id=1, source_target_pairs={{0,3},{1,0},{2,1},{3,2},{4,7},{5,4},{6,5},{7,6},{8,11},{9,8},{10,9... | collective-permute-start | bytes 319496 | tf_op jit(solution)/shard_map/ppermute | solution.py:151
  85.5 1.5 collective-permute-start.10
  87.0 0.8 collective-permute-start.9
  87.8 0.0 collective-permute-done.11.c
  87.8 3.2 %collective-permute-done.10.b = bf16[64,832]{1,0:T(8,128)(2,1)S(1)} collective-permute-done((bf16[64,832]{1,0:T(8,128)(2,1)S(1)}, bf16[64,832]{1,0:T(8,128)(2,1)S(1)}, u32[]{:S(2)}, u32[]{:S(2)}) %collective-permute-start.10) | collective-permute-done | bytes 106528 | tf_op jit(solution)/shard_map/ppermute | solution.py:151
  91.0 3.0 %collective-permute-done.9.a = bf16[64,832]{1,0:T(8,128)(2,1)S(1)} collective-permute-done((bf16[64,832]{1,0:T(8,128)(2,1)S(1)}, bf16[64,832]{1,0:T(8,128)(2,1)S(1)}, u32[]{:S(2)}, u32[]{:S(2)}) %collective-permute-start.9) | collective-permute-done | bytes 106528 | tf_op jit(solution)/shard_map/ppermute | solution.py:151
  94.1 3.5 %shard_map.119 = (f32[64,640]{1,0:T(8,128)}, f32[64,1024]{1,0:T(8,128)}, f32[32,16,128]{2,1,0:T(8,128)S(1)}, f32[32,16,128]{2,1,0:T(8,128)S(1)}) custom-call(s32[1]{0:T(128)} %bitcast.place, f32[64,640]{1,0:T(8,128)S(1)} %get-tuple-element.29.product, f32[64,64]{1,0:T(8,128)S(1)} %get-tuple-element.30.gram, bf16[64,832]{1,0:T(8,128)(2,1)S(1)} %collective-permute-done.9.a, ...), custom_call_target="tpu_custom_call" | custom-call | tf_op jit(solution)/shard_map/pallas_call | solution.py:191
  97.6 0.9 collective-permute-start.12
  98.5 1.2 collective-permute-done.12
  99.7 14.9 %all_to_all.37.parts = f32[32,16,128]{2,1,0:T(8,128)S(1)} all-to-all(f32[32,16,128]{2,1,0:T(8,128)S(1)} %add.18), channel_id=1, replica_groups=mesh['chip'=32,'core'=2,'snp'=4] {'chip'}, dimensions={0} | all-to-all | bytes 524288 | tf_op jit(solution)/shard_map/all_to_all | solution.py:157
  114.6 0.1 shard_map.120
  114.7 15.0 %all_to_all.38.mine = f32[32,16,128]{2,1,0:T(8,128)S(1)} all-to-all(f32[32,16,128]{2,1,0:T(8,128)S(1)} %shard_map.120), channel_id=1, replica_groups=mesh['chip'=32,'core'=2,'snp'=4] {'chip'}, dimensions={0} | all-to-all | bytes 524288 | tf_op jit(solution)/shard_map/all_to_all | solution.py:159
  129.7 3.3 %collective-permute-start.13 = (f32[32,16,128]{2,1,0:T(8,128)S(1)}, f32[32,16,128]{2,1,0:T(8,128)S(1)}, u32[]{:S(2)}, u32[]{:S(2)}) collective-permute-start(f32[32,16,128]{2,1,0:T(8,128)S(1)} %all_to_all.38.mine), channel_id=1, source_target_pairs={{0,4},{4,0},{1,5},{5,1},{2,6},{6,2},{3,7},{7,3},{8,12},{12,8},{9,1... | collective-permute-start | bytes 786440 | tf_op jit(solution)/shard_map/ppermute | solution.py:147
  133.0 1.2 collective-permute-done.13.other
  134.2 3.1 %shard_map.121 = (f32[64,1024]{1,0:T(8,128)S(1)}, f32[64,640]{1,0:T(8,128)S(1)}, f32[64,64]{1,0:T(8,128)S(1)}, bf16[64,832]{1,0:T(8,128)(2,1)S(1)}) custom-call(s32[1]{0:T(128)} %bitcast.place, f32[32,16,128]{2,1,0:T(8,128)S(1)} %all_to_all.38.mine, f32[32,16,128]{2,1,0:T(8,128)S(1)} %collective-permute-done.13.other, bf16[640,1024]{1,0:T(8,128)(2,1)S(1)} %shard_map.115.x), custom_call_target="tpu_custom_call" | custom-call | tf_op jit(solution)/shard_map/pallas_call | solution.py:191
  137.2 0.3 collective-permute-start.16
  137.6 1.6 collective-permute-start.15
  139.2 0.4 collective-permute-start.14
  139.6 2.0 %collective-permute-done.16.c = bf16[64,832]{1,0:T(8,128)(2,1)S(1)} collective-permute-done((bf16[64,832]{1,0:T(8,128)(2,1)S(1)}, bf16[64,832]{1,0:T(8,128)(2,1)S(1)}, u32[]{:S(2)}, u32[]{:S(2)}) %collective-permute-start.16) | collective-permute-done | bytes 106528 | tf_op jit(solution)/shard_map/ppermute | solution.py:151
  141.6 1.5 collective-permute-done.15.b
  143.1 3.0 %collective-permute-done.14.a = bf16[64,832]{1,0:T(8,128)(2,1)S(1)} collective-permute-done((bf16[64,832]{1,0:T(8,128)(2,1)S(1)}, bf16[64,832]{1,0:T(8,128)(2,1)S(1)}, u32[]{:S(2)}, u32[]{:S(2)}) %collective-permute-start.14) | collective-permute-done | bytes 106528 | tf_op jit(solution)/shard_map/ppermute | solution.py:151
  146.2 3.4 %shard_map.122 = (f32[64,640]{1,0:T(8,128)S(1)}, f32[64,1024]{1,0:T(8,128)}, f32[32,16,128]{2,1,0:T(8,128)S(1)}, f32[32,16,128]{2,1,0:T(8,128)S(1)}) custom-call(s32[1]{0:T(128)} %bitcast.place, f32[64,640]{1,0:T(8,128)S(1)} %get-tuple-element.35.product, f32[64,64]{1,0:T(8,128)S(1)} %get-tuple-element.36.gram, ...), custom_call_target="tpu_custom_call" | custom-call | tf_op jit(solution)/shard_map/pallas_call | solution.py:191
  149.6 0.9 collective-permute-start.17
  150.5 1.2 collective-permute-done.17
  151.7 14.9 %all_to_all.39.parts = f32[32,16,128]{2,1,0:T(8,128)S(1)} all-to-all(f32[32,16,128]{2,1,0:T(8,128)S(1)} %add.19), channel_id=1, replica_groups=mesh['chip'=32,'core'=2,'snp'=4] {'chip'}, dimensions={0} | all-to-all | bytes 524288 | tf_op jit(solution)/shard_map/all_to_all | solution.py:157
  166.6 0.1 shard_map.123
  166.7 15.0 %all_to_all.40.mine = f32[32,16,128]{2,1,0:T(8,128)S(1)} all-to-all(f32[32,16,128]{2,1,0:T(8,128)S(1)} %shard_map.123), channel_id=1, replica_groups=mesh['chip'=32,'core'=2,'snp'=4] {'chip'}, dimensions={0} | all-to-all | bytes 524288 | tf_op jit(solution)/shard_map/all_to_all | solution.py:159
  181.7 3.3 %collective-permute-start.18 = (f32[32,16,128]{2,1,0:T(8,128)S(1)}, f32[32,16,128]{2,1,0:T(8,128)S(1)}, u32[]{:S(2)}, u32[]{:S(2)}) collective-permute-start(f32[32,16,128]{2,1,0:T(8,128)S(1)} %all_to_all.40.mine), channel_id=1, source_target_pairs={{0,4},{4,0},{1,5},{5,1},{2,6},{6,2},{3,7},{7,3},{8,12},{12,8},{9,1... | collective-permute-start | bytes 786440 | tf_op jit(solution)/shard_map/ppermute | solution.py:147
  185.0 1.2 collective-permute-done.18.other
  186.1 3.2 %shard_map.124 = (f32[64,640]{1,0:T(8,128)}, f32[64,1024]{1,0:T(8,128)}) custom-call(s32[1]{0:T(128)} %bitcast.place, f32[32,16,128]{2,1,0:T(8,128)S(1)} %all_to_all.40.mine, f32[32,16,128]{2,1,0:T(8,128)S(1)} %collective-permute-done.18.other, f32[64,640]{1,0:T(8,128)S(1)} %get-tuple-element.41.samples), custom_call_target="tpu_custom_call" | custom-call | tf_op jit(solution)/shard_map/pallas_call | solution.py:191
  (16 shorter events, 0.1 us)
Async XLA Ops:
  0.6 6.6 %collective-permute-start.3 = (f32[16,20]{1,0:T(8,128)}, f32[16,20]{1,0:T(8,128)S(1)}, u32[]{:S(2)}, u32[]{:S(2)}) collective-permute-start(f32[16,20]{1,0:T(8,128)} %mine.1), channel_id=1, source_target_pairs={{0,4},{4,0},{1,5},{5,1},{2,6},{6,2},{3,7},{7,3},{8,12},{12,8},{9,1... | collective-permute-start | bytes 3848 | tf_op jit(solution)/shard_map/ppermute | solution.py:147
  4.0 3.2 %copy-start.4 = (f32[16,20]{1,0:T(8,128)S(1)}, f32[16,20]{1,0:T(8,128)}, u32[]{:S(2)}) copy-start(f32[16,20]{1,0:T(8,128)} %mine.1) | copy-start | bytes 3844
  4.0 24.4 %copy-start.1 = (bf16[1024,64]{0,1:T(8,128)(2,1)S(1)}, bf16[1024,64]{0,1:T(8,128)(2,1)}, u32[]{:S(2)}) copy-start(bf16[1024,64]{0,1:T(8,128)(2,1)} %param.14) | copy-start | bytes 393220
  4.0 28.8 %copy-start.2 = (f32[640,20]{0,1:T(8,128)S(1)}, f32[640,20]{0,1:T(8,128)}, u32[]{:S(2)}) copy-start(f32[640,20]{0,1:T(8,128)} %param.11) | copy-start | bytes 153604
  4.0 28.8 %copy-start.5 = (s32[12]{0:T(128)S(1)}, s32[12]{0:T(128)}, u32[]{:S(2)}) copy-start(s32[12]{0:T(128)} %sizes.3) | copy-start | bytes 148
  4.0 28.8 %copy-start.8 = (f32[20]{0:T(128)S(1)}, f32[20]{0:T(128)}, u32[]{:S(2)}) copy-start(f32[20]{0:T(128)} %scale.3) | copy-start | bytes 244
  7.2 0.7 copy-start.6
  9.2 19.2 %all-to-all-start = ((f32[32,8,128]{2,1,0:T(8,128)}), f32[32,8,128]{2,1,0:T(8,128)S(1)}, u32[]{:S(2)}, u32[]{:S(2)}) async-start(f32[32,8,128]{2,1,0:T(8,128)} %shard_map.113), calls=%async_computation | async-start | bytes 262144 | tf_op jit(solution)/shard_map/all_to_all | solution.py:307
  18.5 13.6 %collective-permute-start.2 = (f32[64,640]{1,0:T(8,128)}, f32[64,640]{1,0:T(8,128)S(1)}, u32[]{:S(2)}, u32[]{:S(2)}) collective-permute-start(f32[64,640]{1,0:T(8,128)} %get-tuple-element.25.own), channel_id=1, source_target_pairs={{0,3},{1,0},{2,1},{3,2},{4,7},{5,4},{6,5},{7,6},{8,11},{9,8},{10,9... | collective-permute-start | bytes 491528 | tf_op jit(solution)/shard_map/ppermute | solution.py:151
  21.3 16.4 %collective-permute-start.1 = (f32[64,640]{1,0:T(8,128)}, f32[64,640]{1,0:T(8,128)S(1)}, u32[]{:S(2)}, u32[]{:S(2)}) collective-permute-start(f32[64,640]{1,0:T(8,128)} %get-tuple-element.25.own), channel_id=1, source_target_pairs={{0,2},{1,3},{2,0},{3,1},{4,6},{5,7},{6,4},{7,5},{8,10},{9,11},{10,... | collective-permute-start | bytes 491528 | tf_op jit(solution)/shard_map/ppermute | solution.py:151
  21.6 16.1 %collective-permute-start = (f32[64,640]{1,0:T(8,128)}, f32[64,640]{1,0:T(8,128)S(1)}, u32[]{:S(2)}, u32[]{:S(2)}) collective-permute-start(f32[64,640]{1,0:T(8,128)} %get-tuple-element.25.own), channel_id=1, source_target_pairs={{0,1},{1,2},{2,3},{3,0},{4,5},{5,6},{6,7},{7,4},{8,9},{9,10},{10,1... | collective-permute-start | bytes 491528 | tf_op jit(solution)/shard_map/ppermute | solution.py:151
  28.9 8.8 %collective-permute-start.6 = (f32[64,128]{1,0:T(8,128)S(1)}, f32[64,128]{1,0:T(8,128)S(1)}, u32[]{:S(2)}, u32[]{:S(2)}) collective-permute-start(f32[64,128]{1,0:T(8,128)S(1)} %shard_map.114.q0), channel_id=1, source_target_pairs={{0,3},{1,0},{2,1},{3,2},{4,7},{5,4},{6,5},{7,6},{8,11},{9,8},{10,9... | collective-permute-start | bytes 98312 | tf_op jit(solution)/shard_map/ppermute | solution.py:151
  31.7 6.0 %collective-permute-start.5 = (f32[64,128]{1,0:T(8,128)S(1)}, f32[64,128]{1,0:T(8,128)S(1)}, u32[]{:S(2)}, u32[]{:S(2)}) collective-permute-start(f32[64,128]{1,0:T(8,128)S(1)} %shard_map.114.q0), channel_id=1, source_target_pairs={{0,2},{1,3},{2,0},{3,1},{4,6},{5,7},{6,4},{7,5},{8,10},{9,11},{10,... | collective-permute-start | bytes 98312 | tf_op jit(solution)/shard_map/ppermute | solution.py:151
  32.1 5.6 %collective-permute-start.4 = (f32[64,128]{1,0:T(8,128)S(1)}, f32[64,128]{1,0:T(8,128)S(1)}, u32[]{:S(2)}, u32[]{:S(2)}) collective-permute-start(f32[64,128]{1,0:T(8,128)S(1)} %shard_map.114.q0), channel_id=1, source_target_pairs={{0,1},{1,2},{2,3},{3,0},{4,5},{5,6},{6,7},{7,4},{8,9},{9,10},{10,1... | collective-permute-start | bytes 98312 | tf_op jit(solution)/shard_map/ppermute | solution.py:151
  32.8 1.3 copy-start
  34.1 0.7 copy-start.7
  34.8 3.0 %copy-start.3 = (f32[64,640]{1,0:T(8,128)S(1)}, f32[64,640]{1,0:T(8,128)}, u32[]{:S(2)}) copy-start(f32[64,640]{1,0:T(8,128)} %get-tuple-element.25.own) | copy-start | bytes 491524
  40.0 3.4 %collective-permute-start.7 = (f32[32,16,128]{2,1,0:T(8,128)S(1)}, f32[32,16,128]{2,1,0:T(8,128)S(1)}, u32[]{:S(2)}, u32[]{:S(2)}) collective-permute-start(f32[32,16,128]{2,1,0:T(8,128)S(1)} %get-tuple-element.28), channel_id=1, source_target_pairs={{0,4},{4,0},{1,5},{5,1},{2,6},{6,2},{3,7},{7,3},{8,12},{12,8},{9,1... | collective-permute-start | bytes 786440 | tf_op jit(solution)/shard_map/ppermute | solution.py:147
  75.1 4.5 %collective-permute-start.8 = (f32[32,16,128]{2,1,0:T(8,128)S(1)}, f32[32,16,128]{2,1,0:T(8,128)S(1)}, u32[]{:S(2)}, u32[]{:S(2)}) collective-permute-start(f32[32,16,128]{2,1,0:T(8,128)S(1)} %all_to_all.36.mine), channel_id=1, source_target_pairs={{0,4},{4,0},{1,5},{5,1},{2,6},{6,2},{3,7},{7,3},{8,12},{12,8},{9,1... | collective-permute-start | bytes 786440 | tf_op jit(solution)/shard_map/ppermute | solution.py:147
  82.6 5.2 %collective-permute-start.11 = (bf16[64,832]{1,0:T(8,128)(2,1)S(1)}, bf16[64,832]{1,0:T(8,128)(2,1)S(1)}, u32[]{:S(2)}, u32[]{:S(2)}) collective-permute-start(bf16[64,832]{1,0:T(8,128)(2,1)S(1)} %get-tuple-element.31), channel_id=1, source_target_pairs={{0,3},{1,0},{2,1},{3,2},{4,7},{5,4},{6,5},{7,6},{8,11},{9,8},{10,9... | collective-permute-start | bytes 319496 | tf_op jit(solution)/shard_map/ppermute | solution.py:151
  85.5 5.5 %collective-permute-start.10 = (bf16[64,832]{1,0:T(8,128)(2,1)S(1)}, bf16[64,832]{1,0:T(8,128)(2,1)S(1)}, u32[]{:S(2)}, u32[]{:S(2)}) collective-permute-start(bf16[64,832]{1,0:T(8,128)(2,1)S(1)} %get-tuple-element.31), channel_id=1, source_target_pairs={{0,2},{1,3},{2,0},{3,1},{4,6},{5,7},{6,4},{7,5},{8,10},{9,11},{10,... | collective-permute-start | bytes 319496 | tf_op jit(solution)/shard_map/ppermute | solution.py:151
  87.0 7.0 %collective-permute-start.9 = (bf16[64,832]{1,0:T(8,128)(2,1)S(1)}, bf16[64,832]{1,0:T(8,128)(2,1)S(1)}, u32[]{:S(2)}, u32[]{:S(2)}) collective-permute-start(bf16[64,832]{1,0:T(8,128)(2,1)S(1)} %get-tuple-element.31), channel_id=1, source_target_pairs={{0,1},{1,2},{2,3},{3,0},{4,5},{5,6},{6,7},{7,4},{8,9},{9,10},{10,1... | collective-permute-start | bytes 319496 | tf_op jit(solution)/shard_map/ppermute | solution.py:151
  97.6 2.1 %collective-permute-start.12 = (f32[32,16,128]{2,1,0:T(8,128)S(1)}, f32[32,16,128]{2,1,0:T(8,128)S(1)}, u32[]{:S(2)}, u32[]{:S(2)}) collective-permute-start(f32[32,16,128]{2,1,0:T(8,128)S(1)} %get-tuple-element.34), channel_id=1, source_target_pairs={{0,4},{4,0},{1,5},{5,1},{2,6},{6,2},{3,7},{7,3},{8,12},{12,8},{9,1... | collective-permute-start | bytes 786440 | tf_op jit(solution)/shard_map/ppermute | solution.py:147
  129.7 4.5 %collective-permute-start.13 = (f32[32,16,128]{2,1,0:T(8,128)S(1)}, f32[32,16,128]{2,1,0:T(8,128)S(1)}, u32[]{:S(2)}, u32[]{:S(2)}) collective-permute-start(f32[32,16,128]{2,1,0:T(8,128)S(1)} %all_to_all.38.mine), channel_id=1, source_target_pairs={{0,4},{4,0},{1,5},{5,1},{2,6},{6,2},{3,7},{7,3},{8,12},{12,8},{9,1... | collective-permute-start | bytes 786440 | tf_op jit(solution)/shard_map/ppermute | solution.py:147
  137.2 4.4 %collective-permute-start.16 = (bf16[64,832]{1,0:T(8,128)(2,1)S(1)}, bf16[64,832]{1,0:T(8,128)(2,1)S(1)}, u32[]{:S(2)}, u32[]{:S(2)}) collective-permute-start(bf16[64,832]{1,0:T(8,128)(2,1)S(1)} %get-tuple-element.37), channel_id=1, source_target_pairs={{0,3},{1,0},{2,1},{3,2},{4,7},{5,4},{6,5},{7,6},{8,11},{9,8},{10,9... | collective-permute-start | bytes 319496 | tf_op jit(solution)/shard_map/ppermute | solution.py:151
  137.6 5.6 %collective-permute-start.15 = (bf16[64,832]{1,0:T(8,128)(2,1)S(1)}, bf16[64,832]{1,0:T(8,128)(2,1)S(1)}, u32[]{:S(2)}, u32[]{:S(2)}) collective-permute-start(bf16[64,832]{1,0:T(8,128)(2,1)S(1)} %get-tuple-element.37), channel_id=1, source_target_pairs={{0,2},{1,3},{2,0},{3,1},{4,6},{5,7},{6,4},{7,5},{8,10},{9,11},{10,... | collective-permute-start | bytes 319496 | tf_op jit(solution)/shard_map/ppermute | solution.py:151
  139.2 7.0 %collective-permute-start.14 = (bf16[64,832]{1,0:T(8,128)(2,1)S(1)}, bf16[64,832]{1,0:T(8,128)(2,1)S(1)}, u32[]{:S(2)}, u32[]{:S(2)}) collective-permute-start(bf16[64,832]{1,0:T(8,128)(2,1)S(1)} %get-tuple-element.37), channel_id=1, source_target_pairs={{0,1},{1,2},{2,3},{3,0},{4,5},{5,6},{6,7},{7,4},{8,9},{9,10},{10,1... | collective-permute-start | bytes 319496 | tf_op jit(solution)/shard_map/ppermute | solution.py:151
  149.6 2.1 %collective-permute-start.17 = (f32[32,16,128]{2,1,0:T(8,128)S(1)}, f32[32,16,128]{2,1,0:T(8,128)S(1)}, u32[]{:S(2)}, u32[]{:S(2)}) collective-permute-start(f32[32,16,128]{2,1,0:T(8,128)S(1)} %get-tuple-element.40), channel_id=1, source_target_pairs={{0,4},{4,0},{1,5},{5,1},{2,6},{6,2},{3,7},{7,3},{8,12},{12,8},{9,1... | collective-permute-start | bytes 786440 | tf_op jit(solution)/shard_map/ppermute | solution.py:147
  181.7 4.5 %collective-permute-start.18 = (f32[32,16,128]{2,1,0:T(8,128)S(1)}, f32[32,16,128]{2,1,0:T(8,128)S(1)}, u32[]{:S(2)}, u32[]{:S(2)}) collective-permute-start(f32[32,16,128]{2,1,0:T(8,128)S(1)} %all_to_all.40.mine), channel_id=1, source_target_pairs={{0,4},{4,0},{1,5},{5,1},{2,6},{6,2},{3,7},{7,3},{8,12},{12,8},{9,1... | collective-permute-start | bytes 786440 | tf_op jit(solution)/shard_map/ppermute | solution.py:147
